TPU v7x, 512 devices: a whole 4x8x8 slice. The times are simulated.
512 devices in a mesh: ctx: 64 (over z_lo, y, core), head: 8 (over z_hi, x).
Axes of the slice: x: 4, y: 8, z: 8 (z_hi: 2, z_lo: 4; z = z_hi * 4 + z_lo), core: 2. Of those that a mesh axis runs over, the one named last changes fastest.
Arguments:
- frozen_queries: bfloat16 [8192, 12288], P('ctx', 'head'), may hold values from -20.4 to 20.4
- query_latent_rows: bfloat16 [8192, 1536], P('ctx'), may hold values from -6 to 6
- key_value_latent: bfloat16 [8192, 576], P('ctx'), may hold values from -20.4 to 20.4
- block_starts: int32 [64, 2], P('ctx'), may hold values from 0 to 960, as said below
- latent_up_weight: bfloat16 [512, 16384], P(None, 'head'), may hold values from -0.25 to 0.25
- query_adapter_first: bfloat16 [1536, 32], replicated, may hold values from -0.15625 to 0.15625
- query_adapter_second: bfloat16 [32, 12288], P(None, 'head'), may hold values from -1 to 1
- output_adapter_first: bfloat16 [8192, 32], P('head'), may hold values from -0.0625 to 0.0625
- output_adapter_second: bfloat16 [32, 2560], replicated, may hold values from -1 to 1
- frozen_output_weight: bfloat16 [8192, 2560], P('head', 'ctx'), may hold values from -0.0625 to 0.0625
- output_cotangent: bfloat16 [8192, 2560], P('ctx'), may hold values from -0.1875 to 0.1875
Outputs:
- grad_qa: float32 [1536, 32], replicated
- grad_qb: float32 [32, 12288], P(None, 'head')
- grad_oa: float32 [8192, 32], P('head')
- grad_ob: float32 [32, 2560], P(None, 'ctx')
Inputs may be any that keep to these rules, and one draw needn't show every extreme that they name: For c < 8, each of the 8 groups of one sequence holds block_starts = (c * 64, (15 - c) * 64), every c once per sequence.
All inputs are finite; a program needn't handle non-finite values.
Results may differ from a plain program's by a relative error of at most 0.02.
The roundings to bfloat16 on the way count: a program that leaves them out, or rounds other values in their place, can miss the bound.
Values may be sent and summed in bfloat16 or wider, within the bound.
A program may use at most 128 MiB of HBM per device.

v0:
```python
import jax
import jax.numpy as jnp
from jax import lax
from jax.sharding import PartitionSpec as P

PLAIN_WIDTH = 128
ROTARY_WIDTH = 64
VALUE_WIDTH = 128
KVL = 512
SPAN = 8


ROPE_BASE = 10000.0


def passed_along(value, axis, steps):
    count = lax.axis_size(axis)
    pairs = [(source, (source + steps) % count) for source in range(count)]
    return lax.ppermute(value, axis, pairs)


def rotate(vectors, positions, sign):
    half_width = vectors.shape[-1] // 2
    freq = ROPE_BASE ** (-jnp.arange(half_width, dtype=jnp.float32) * 2.0 / vectors.shape[-1])
    angle = positions.astype(jnp.float32)[..., None] * freq
    angle = angle.reshape(
        positions.shape + (1,) * (vectors.ndim - positions.ndim - 1) + (half_width,)
    )
    cosine = jnp.cos(angle)
    sine = jnp.sin(angle) * sign
    first = vectors[..., :half_width]
    second = vectors[..., half_width:]
    return jnp.concatenate([first * cosine - second * sine, second * cosine + first * sine], -1)


def block_positions(offsets, half_rows):
    steps = jnp.arange(half_rows, dtype=jnp.int32)
    return jnp.concatenate([offsets[0] + steps, offsets[1] + steps])


def expand_block(latent_rows, latent_up_weight, positions):
    kv_up = jnp.dot(
        latent_rows[:, :KVL], latent_up_weight, preferred_element_type=jnp.float32
    ).astype(jnp.bfloat16)
    rope_key = rotate(latent_rows[:, KVL:].astype(jnp.float32), positions, 1.0).astype(jnp.bfloat16)
    return jnp.concatenate([kv_up, rope_key], -1)


def block_scores(query_full, block, head_number):
    split = head_number * (PLAIN_WIDTH + VALUE_WIDTH)
    kv_heads = block[:, :split].reshape(block.shape[0], head_number, PLAIN_WIDTH + VALUE_WIDTH)
    nope_part = jnp.einsum(
        "qhd,khd->hqk",
        query_full[..., :PLAIN_WIDTH],
        kv_heads[..., :PLAIN_WIDTH],
        preferred_element_type=jnp.float32,
    )
    rope_part = jnp.einsum(
        "qhd,kd->hqk",
        query_full[..., PLAIN_WIDTH:],
        block[:, split:],
        preferred_element_type=jnp.float32,
    )
    return nope_part + rope_part


def contract_rows(left, right):
    return lax.dot_general(
        left, right, (((0,), (0,)), ((), ())), preferred_element_type=jnp.float32
    )


def columns_contract(left, right):
    return lax.dot_general(
        left, right, (((1,), (1,)), ((), ())), preferred_element_type=jnp.float32
    )


def body(
    frozen_queries,
    query_latent_rows,
    key_value_latent,
    block_starts,
    latent_up_weight,
    query_adapter_first,
    query_adapter_second,
    output_adapter_first,
    output_adapter_second,
    frozen_output_weight,
    output_cotangent,
):
    token_rows = frozen_queries.shape[0]
    half_rows = token_rows // 2
    per_head_width = PLAIN_WIDTH + ROTARY_WIDTH
    head_number = query_adapter_second.shape[1] // per_head_width
    score_scale = per_head_width ** (-0.5)
    axis_count = lax.axis_size("ctx")
    stride = axis_count // SPAN
    axis_place = lax.axis_index("ctx")
    all_offsets = lax.all_gather(block_starts, "ctx", axis=0, tiled=True)
    own_positions = block_positions(block_starts[0], half_rows)
    query_rank_rows = jnp.dot(
        query_latent_rows, query_adapter_first, preferred_element_type=jnp.float32
    ).astype(jnp.bfloat16)
    query_full = frozen_queries.astype(jnp.float32) + jnp.dot(
        query_rank_rows, query_adapter_second, preferred_element_type=jnp.float32
    )
    query_full = query_full.reshape(token_rows, head_number, per_head_width)
    query_full = jnp.concatenate(
        [query_full[..., :PLAIN_WIDTH], rotate(query_full[..., PLAIN_WIDTH:], own_positions, 1.0)],
        -1,
    ).astype(jnp.bfloat16)

    def prepare(block, positions):
        return expand_block(block, latent_up_weight, positions)

    collected = []

    def take(block, distance):
        source = (axis_place - distance * stride) % axis_count
        source_offsets = lax.dynamic_index_in_dim(all_offsets, source, 0, keepdims=False)
        positions = block_positions(source_offsets, half_rows)
        expanded = prepare(block, positions)
        collected.append((expanded, positions, block_scores(query_full, expanded, head_number)))

    take(key_value_latent, 0)
    moving = key_value_latent
    for hop in range(1, SPAN):
        moving = passed_along(moving, "ctx", stride)
        take(moving, hop)
    kv_all = jnp.concatenate([entry[0] for entry in collected], 0)
    key_positions = jnp.concatenate([entry[1] for entry in collected], 0)
    scores = jnp.concatenate([entry[2] for entry in collected], -1) * score_scale
    causal = key_positions[None, :] <= own_positions[:, None]
    scores = jnp.where(causal[None], scores, -jnp.inf)
    top = jnp.max(scores, -1, keepdims=True)
    expo = jnp.exp(scores - top)
    weights = (expo / jnp.sum(expo, -1, keepdims=True)).astype(jnp.bfloat16)
    split = head_number * (PLAIN_WIDTH + VALUE_WIDTH)
    key_count = kv_all.shape[0]
    kv_heads = kv_all[:, :split].reshape(key_count, head_number, PLAIN_WIDTH + VALUE_WIDTH)
    key_nope = kv_heads[..., :PLAIN_WIDTH]
    values = kv_heads[..., PLAIN_WIDTH:]
    rope_keys = kv_all[:, split:]
    attended_values = jnp.einsum(
        "hqk,khv->qhv", weights, values, preferred_element_type=jnp.float32
    ).astype(jnp.bfloat16)
    attended_flattened = attended_values.reshape(token_rows, head_number * VALUE_WIDTH)
    output_partial_sum = jnp.dot(
        attended_flattened, output_adapter_first, preferred_element_type=jnp.float32
    )
    output_rank_rows = lax.psum(output_partial_sum, "head").astype(jnp.bfloat16)
    output_rank_gradient = columns_contract(output_cotangent, output_adapter_second).astype(
        jnp.bfloat16
    )
    grad_ob = lax.psum_scatter(
        contract_rows(output_rank_rows, output_cotangent), "ctx", scatter_dimension=1, tiled=True
    )
    grad_oa = lax.psum(contract_rows(attended_flattened, output_rank_gradient), "ctx")
    frozen_query_gradient = columns_contract(
        output_cotangent, lax.all_gather(frozen_output_weight, "ctx", axis=1, tiled=True)
    )
    attended_gradient = (
        (frozen_query_gradient + columns_contract(output_rank_gradient, output_adapter_first))
        .astype(jnp.bfloat16)
        .reshape(token_rows, head_number, VALUE_WIDTH)
    )
    d_prob = jnp.einsum(
        "qhv,khv->hqk", attended_gradient, values, preferred_element_type=jnp.float32
    )
    weights_wide = weights.astype(jnp.float32)
    delta = jnp.sum(weights_wide * d_prob, -1, keepdims=True)
    d_score = (weights_wide * (d_prob - delta) * score_scale).astype(jnp.bfloat16)
    dq_nope = jnp.einsum("hqk,khd->qhd", d_score, key_nope, preferred_element_type=jnp.float32)
    dq_rope = jnp.einsum("hqk,kd->qhd", d_score, rope_keys, preferred_element_type=jnp.float32)
    dq_rope = rotate(dq_rope, own_positions, -1.0)
    query_gradient = (
        jnp.concatenate([dq_nope, dq_rope], -1)
        .reshape(token_rows, head_number * per_head_width)
        .astype(jnp.bfloat16)
    )
    qb_term = contract_rows(query_rank_rows, query_gradient)
    query_adapter_gradient = lax.psum(
        columns_contract(query_gradient, query_adapter_second), "head"
    ).astype(jnp.bfloat16)
    qa_term = contract_rows(query_latent_rows, query_adapter_gradient)
    grad_qb, grad_qa = lax.psum((qb_term, qa_term), "ctx")
    return (grad_qa, grad_qb, grad_oa, grad_ob)


def solution(mesh):
    return jax.shard_map(
        body,
        mesh=mesh,
        in_specs=(
            P("ctx", "head"),
            P("ctx", None),
            P("ctx", None),
            P("ctx", None),
            P(None, "head"),
            P(),
            P(None, "head"),
            P("head", None),
            P(),
            P("head", "ctx"),
            P("ctx", None),
        ),
        out_specs=(P(), P(None, "head"), P("head", None), P(None, "ctx")),
        check_vma=False,
    )
```

profile of v0, /device:TPU:1, one launch (start us, length us, event | category | flops | bytes accessed | tf_op | source)
XLA Modules:
  0.0 902.7 jit_solution(16338640068785759681)
XLA Ops:
  7.3 8.5 collective-permute-start
  18.0 1.4 convolution_convert_fusion.7
  24.4 80.7 %all-gather = s32[64,1,2]{2,1,0:T(1,128)} all-gather(s32[1,1,2]{2,1,0:T(1,128)S(1)} %bitcast.209), channel_id=1, replica_groups=mesh['ctx'=64,'head'=8] {'ctx'}, dimensions={0}, use_global_device_ids=true | all-gather | bytes 520 | tf_op jit(solution)/shard_map/all_gather | solution.py:100
  123.5 2.0 fusion.62
  131.0 1.8 convolution_convert_fusion.8
  139.2 1.5 fusion.129
  140.7 1.4 copy.115
  143.5 1.9 concatenate.147
  145.4 1.9 constant_dynamic-update-slice_fusion.7
  148.7 1.9 concatenate.149
  150.6 2.0 constant_dynamic-update-slice_fusion.6
  152.6 1.9 collective-permute-start.1
  154.5 2.0 fusion.60
  156.5 10.0 %collective-permute-done.1 = bf16[128,576]{0,1:T(8,128)(2,1)S(1)} collective-permute-done((bf16[128,576]{0,1:T(8,128)(2,1)}, bf16[128,576]{0,1:T(8,128)(2,1)S(1)}, u32[]{:S(2)}, u32[]{:S(2)}) %collective-permute-start.1) | collective-permute-done | bytes 147488 | tf_op jit(solution)/shard_map/ppermute | solution.py:19
  168.2 1.9 collective-permute-start.2
  170.2 11.2 %collective-permute-done.2 = bf16[128,576]{0,1:T(8,128)(2,1)S(1)} collective-permute-done((bf16[128,576]{0,1:T(8,128)(2,1)S(1)}, bf16[128,576]{0,1:T(8,128)(2,1)S(1)}, u32[]{:S(2)}, u32[]{:S(2)}) %collective-permute-start.2) | collective-permute-done | bytes 147488 | tf_op jit(solution)/shard_map/ppermute | solution.py:19
  183.1 1.9 collective-permute-start.3
  185.0 11.9 %collective-permute-done.3 = bf16[128,576]{0,1:T(8,128)(2,1)S(1)} collective-permute-done((bf16[128,576]{0,1:T(8,128)(2,1)S(1)}, bf16[128,576]{0,1:T(8,128)(2,1)S(1)}, u32[]{:S(2)}, u32[]{:S(2)}) %collective-permute-start.3) | collective-permute-done | bytes 147488 | tf_op jit(solution)/shard_map/ppermute | solution.py:19
  199.9 1.4 copy.119
  201.3 1.4 copy.120
  207.0 1.9 concatenate.151
  208.9 1.9 concatenate.153
  210.7 1.9 concatenate.155
  212.6 1.9 collective-permute-start.4
  214.5 1.9 constant_dynamic-update-slice_fusion.5
  216.5 1.9 constant_dynamic-update-slice_fusion.4
  218.4 1.9 constant_dynamic-update-slice_fusion.3
  220.3 1.9 fusion.54
  222.3 3.1 collective-permute-done.4
  226.0 1.9 collective-permute-start.5
  228.9 10.8 %collective-permute-done.5 = bf16[128,576]{0,1:T(8,128)(2,1)S(1)} collective-permute-done((bf16[128,576]{0,1:T(8,128)(2,1)S(1)}, bf16[128,576]{0,1:T(8,128)(2,1)S(1)}, u32[]{:S(2)}, u32[]{:S(2)}) %collective-permute-start.5) | collective-permute-done | bytes 147488 | tf_op jit(solution)/shard_map/ppermute | solution.py:19
  240.4 1.9 collective-permute-start.6
  243.4 9.6 %collective-permute-done.6 = bf16[128,576]{0,1:T(8,128)(2,1)S(1)} collective-permute-done((bf16[128,576]{0,1:T(8,128)(2,1)S(1)}, bf16[128,576]{0,1:T(8,128)(2,1)S(1)}, u32[]{:S(2)}, u32[]{:S(2)}) %collective-permute-start.6) | collective-permute-done | bytes 147488 | tf_op jit(solution)/shard_map/ppermute | solution.py:19
  262.6 2.5 slice.337
  265.3 1.5 copy.186
  269.5 1.6 fusion.178
  271.0 1.9 fusion.188
  273.4 1.4 copy-done.18
  277.3 3.3 fusion.197
  280.9 2.7 fusion.16
  283.6 6.7 fusion.42
  290.4 7.4 fusion.43
  300.0 50.8 %all-reduce.2 = (bf16[128,32]{0,1:T(8,128)(2,1)S(1)}, bf16[128,32]{0,1:T(8,128)(2,1)S(1)}) all-reduce(f32[128,32]{0,1:T(8,128)S(1)} %fusion.200, f32[128,32]{0,1:T(8,128)} %fusion.201), channel_id=1, replica_groups=mesh['ctx'=64,'head'=8] {'head'}, use_global_device_ids=true, to_apply=%region_3.4 | all-reduce | flops 8192 | bytes 49152 | tf_op jit(solution)/shard_map/psum | solution.py:183
  354.6 535.1 %all-reduce.5.cloned.1.call-done = (f32[1536,32]{0,1:T(8,128)}, f32[32,1536]{1,0:T(8,128)}, f32[1024,32]{0,1:T(8,128)}, f32[32,2560]{1,0:T(8,128)}) async-done(((f32[1536,32]{0,1:T(8,128)}, f32[32,1536]{1,0:T(8,128)}, f32[1024,32]{0,1:T(8,128)}, f32[32,2560]{1,0:T(8,128)}), (f32[1536,32]{0,1:T(8,128)}, f32[32,1536]{1,0:T(8,128)}, f32[1024,32]{0,1:T(8,128)}, ...) | async-done | bytes 851984 | tf_op jit(solution)/shard_map/psum | solution.py:187
  889.6 1.4 constant_dynamic-slice_fusion.8
  891.1 1.6 copy.245
  892.7 1.6 copy.246
  894.3 1.6 copy.247
  (281 shorter events, 74.0 us)
Async XLA Ops:
  7.2 10.8 %copy-start = (bf16[512,2048]{1,0:T(8,128)(2,1)S(1)}, bf16[512,2048]{1,0:T(8,128)(2,1)}, u32[]{:S(2)}) copy-start(bf16[512,2048]{1,0:T(8,128)(2,1)} %param.15) | copy-start | bytes 6291460
  7.2 13.1 %copy-start.19 = (bf16[128,1536]{1,0:T(8,128)(2,1)S(1)}, bf16[128,1536]{1,0:T(8,128)(2,1)}, u32[]{:S(2)}) copy-start(bf16[128,1536]{1,0:T(8,128)(2,1)} %param.12) | copy-start | bytes 1179652
  7.2 14.0 %copy-start.21 = (bf16[128,1536]{1,0:T(8,128)(2,1)S(1)}, bf16[128,1536]{1,0:T(8,128)(2,1)}, u32[]{:S(2)}) copy-start(bf16[128,1536]{1,0:T(8,128)(2,1)} %param.11) | copy-start | bytes 1179652
  7.2 16.6 %copy-start.62 = (s32[1,2]{1,0:T(1,128)S(1)}, s32[1,2]{1,0:T(1,128)}, u32[]{:S(2)}) copy-start(s32[1,2]{1,0:T(1,128)} %param.14) | copy-start | bytes 28
  7.2 270.1 %all-gather.3.cloned.1.call-start = ((), (), s32[]{:S(2)}) async-start(), calls=%async_computation | async-start | bytes 5324800 | tf_op jit(solution)/shard_map/all_gather | solution.py:161
  7.3 128.1 %collective-permute-start = (bf16[128,576]{0,1:T(8,128)(2,1)}, bf16[128,576]{0,1:T(8,128)(2,1)}, u32[]{:S(2)}, u32[]{:S(2)}) collective-permute-start(bf16[128,576]{0,1:T(8,128)(2,1)} %param.13), channel_id=1, source_target_pairs={{0,64},{8,72},{16,80},{24,88},{32,96},{40,104},{48,112},{56,120},{... | collective-permute-start | bytes 442376 | tf_op jit(solution)/shard_map/ppermute | solution.py:19
  15.8 873.8 %all-reduce.5.cloned.1.call-start = ((), (), s32[]{:S(2)}) async-start(), calls=%async_computation.1 | async-start | bytes 1703936 | tf_op jit(solution)/shard_map/psum | solution.py:187
  16.0 4.3 copy-start.28
  16.0 5.1 copy-start.22
  18.0 113.1 %copy-start.2 = (bf16[128,2560]{1,0:T(8,128)(2,1)S(1)}, bf16[128,2560]{1,0:T(8,128)(2,1)}, u32[]{:S(2)}) copy-start(bf16[128,2560]{1,0:T(8,128)(2,1)} %param.21) | copy-start | bytes 1966084
  109.0 19.7 %copy-start.70 = (s32[64]{0:T(128)}, s32[64]{0:T(128)S(1)}, u32[]{:S(2)}) copy-start(s32[64]{0:T(128)S(1)} %iota_add_fusion.14) | copy-start | bytes 772
  109.6 19.1 %copy-start.71 = (s32[64]{0:T(128)}, s32[64]{0:T(128)S(1)}, u32[]{:S(2)}) copy-start(s32[64]{0:T(128)S(1)} %iota_add_fusion.15) | copy-start | bytes 772
  110.9 17.8 %copy-start.78 = (s32[64]{0:T(128)}, s32[64]{0:T(128)S(1)}, u32[]{:S(2)}) copy-start(s32[64]{0:T(128)S(1)} %iota_add_fusion.2) | copy-start | bytes 772
  111.5 17.2 %copy-start.79 = (s32[64]{0:T(128)}, s32[64]{0:T(128)S(1)}, u32[]{:S(2)}) copy-start(s32[64]{0:T(128)S(1)} %iota_add_fusion.3) | copy-start | bytes 772
  112.8 15.9 %copy-start.72 = (s32[64]{0:T(128)}, s32[64]{0:T(128)S(1)}, u32[]{:S(2)}) copy-start(s32[64]{0:T(128)S(1)} %iota_add_fusion.6) | copy-start | bytes 772
  113.5 15.3 %copy-start.73 = (s32[64]{0:T(128)}, s32[64]{0:T(128)S(1)}, u32[]{:S(2)}) copy-start(s32[64]{0:T(128)S(1)} %iota_add_fusion.7) | copy-start | bytes 772
  114.7 14.0 %copy-start.74 = (s32[64]{0:T(128)}, s32[64]{0:T(128)S(1)}, u32[]{:S(2)}) copy-start(s32[64]{0:T(128)S(1)} %iota_add_fusion.4) | copy-start | bytes 772
  115.4 13.4 %copy-start.75 = (s32[64]{0:T(128)}, s32[64]{0:T(128)S(1)}, u32[]{:S(2)}) copy-start(s32[64]{0:T(128)S(1)} %iota_add_fusion.5) | copy-start | bytes 772
  130.2 9.0 %copy-start.26 = (f32[128,64]{0,1:T(8,128)S(1)}, f32[128,64]{0,1:T(8,128)}, u32[]{:S(2)}) copy-start(f32[128,64]{0,1:T(8,128)} %slice_convert_fusion.8) | copy-start | bytes 98308
  130.2 9.0 %copy-start.68 = (f32[128]{0:T(128)S(1)}, f32[128]{0:T(128)}, u32[]{:S(2)}) copy-start(f32[128]{0:T(128)} %get-tuple-element.77) | copy-start | bytes 1540
  130.2 9.0 %copy-start.69 = (f32[128]{0:T(128)S(1)}, f32[128]{0:T(128)}, u32[]{:S(2)}) copy-start(f32[128]{0:T(128)} %get-tuple-element.78) | copy-start | bytes 1540
  140.7 26.3 %copy-start.32 = (bf16[128,32]{0,1:T(8,128)(2,1)}, bf16[128,32]{0,1:T(8,128)(2,1)S(1)}, u32[]{:S(2)}) copy-start(bf16[128,32]{0,1:T(8,128)(2,1)S(1)} %get-tuple-element.30) | copy-start | bytes 24580
  140.7 26.3 %copy-start.34 = (bf16[128,32]{0,1:T(8,128)(2,1)}, bf16[128,32]{0,1:T(8,128)(2,1)S(1)}, u32[]{:S(2)}) copy-start(bf16[128,32]{0,1:T(8,128)(2,1)S(1)} %get-tuple-element.31) | copy-start | bytes 24580
  152.6 13.9 %collective-permute-start.1 = (bf16[128,576]{0,1:T(8,128)(2,1)}, bf16[128,576]{0,1:T(8,128)(2,1)S(1)}, u32[]{:S(2)}, u32[]{:S(2)}) collective-permute-start(bf16[128,576]{0,1:T(8,128)(2,1)} %collective-permute-done), channel_id=1, source_target_pairs={{0,64},{8,72},{16,80},{24,88},{32,96},{40,104},{48,112},{56,120},{... | collective-permute-start | bytes 442376 | tf_op jit(solution)/shard_map/ppermute | solution.py:19
  167.0 16.1 %copy-start.5 = (bf16[128,2048]{1,0:T(8,128)(2,1)}, bf16[128,2048]{1,0:T(8,128)(2,1)S(1)}, u32[]{:S(2)}) copy-start(bf16[128,2048]{1,0:T(8,128)(2,1)S(1)} %convolution_convert_fusion.5) | copy-start | bytes 1572868
  168.2 13.1 %collective-permute-start.2 = (bf16[128,576]{0,1:T(8,128)(2,1)S(1)}, bf16[128,576]{0,1:T(8,128)(2,1)S(1)}, u32[]{:S(2)}, u32[]{:S(2)}) collective-permute-start(bf16[128,576]{0,1:T(8,128)(2,1)S(1)} %collective-permute-done.1), channel_id=1, source_target_pairs={{0,64},{8,72},{16,80},{24,88},{32,96},{40,104},{48,112},{56,120},{... | collective-permute-start | bytes 442376 | tf_op jit(solution)/shard_map/ppermute | solution.py:19
  181.8 17.1 %copy-start.60 = (f32[32]{0:T(128)S(1)}, f32[32]{0:T(128)}, u32[]{:S(2)}) copy-start(f32[32]{0:T(128)} %multiply_power_fusion) | copy-start | bytes 388
  181.8 17.1 %copy-start.66 = (f32[128]{0:T(128)S(1)}, f32[128]{0:T(128)}, u32[]{:S(2)}) copy-start(f32[128]{0:T(128)} %get-tuple-element.79) | copy-start | bytes 1540
  181.8 17.1 %copy-start.67 = (f32[128]{0:T(128)S(1)}, f32[128]{0:T(128)}, u32[]{:S(2)}) copy-start(f32[128]{0:T(128)} %get-tuple-element.80) | copy-start | bytes 1540
  181.9 17.1 %copy-start.77 = (f32[128]{0:T(128)S(1)}, f32[128]{0:T(128)}, u32[]{:S(2)}) copy-start(f32[128]{0:T(128)} %add_convert_fusion.6) | copy-start | bytes 1540
  183.1 13.8 %collective-permute-start.3 = (bf16[128,576]{0,1:T(8,128)(2,1)S(1)}, bf16[128,576]{0,1:T(8,128)(2,1)S(1)}, u32[]{:S(2)}, u32[]{:S(2)}) collective-permute-start(bf16[128,576]{0,1:T(8,128)(2,1)S(1)} %collective-permute-done.2), channel_id=1, source_target_pairs={{0,64},{8,72},{16,80},{24,88},{32,96},{40,104},{48,112},{56,120},{... | collective-permute-start | bytes 442376 | tf_op jit(solution)/shard_map/ppermute | solution.py:19
  199.9 25.9 %copy-start.38 = (bf16[128,32]{0,1:T(8,128)(2,1)}, bf16[128,32]{0,1:T(8,128)(2,1)S(1)}, u32[]{:S(2)}) copy-start(bf16[128,32]{0,1:T(8,128)(2,1)S(1)} %get-tuple-element.24) | copy-start | bytes 24580
  199.9 25.9 %copy-start.40 = (bf16[128,32]{0,1:T(8,128)(2,1)}, bf16[128,32]{0,1:T(8,128)(2,1)S(1)}, u32[]{:S(2)}) copy-start(bf16[128,32]{0,1:T(8,128)(2,1)S(1)} %get-tuple-element.25) | copy-start | bytes 24580
  212.6 12.7 %collective-permute-start.4 = (bf16[128,576]{0,1:T(8,128)(2,1)}, bf16[128,576]{0,1:T(8,128)(2,1)S(1)}, u32[]{:S(2)}, u32[]{:S(2)}) collective-permute-start(bf16[128,576]{0,1:T(8,128)(2,1)} %copy-done.25), channel_id=1, source_target_pairs={{0,64},{8,72},{16,80},{24,88},{32,96},{40,104},{48,112},{56,120},{... | collective-permute-start | bytes 442376 | tf_op jit(solution)/shard_map/ppermute | solution.py:19
  225.8 17.6 %copy-start.4 = (bf16[128,2048]{1,0:T(8,128)(2,1)}, bf16[128,2048]{1,0:T(8,128)(2,1)S(1)}, u32[]{:S(2)}) copy-start(bf16[128,2048]{1,0:T(8,128)(2,1)S(1)} %convolution_convert_fusion.2) | copy-start | bytes 1572868
  226.0 13.8 %collective-permute-start.5 = (bf16[128,576]{0,1:T(8,128)(2,1)S(1)}, bf16[128,576]{0,1:T(8,128)(2,1)S(1)}, u32[]{:S(2)}, u32[]{:S(2)}) collective-permute-start(bf16[128,576]{0,1:T(8,128)(2,1)S(1)} %collective-permute-done.4), channel_id=1, source_target_pairs={{0,64},{8,72},{16,80},{24,88},{32,96},{40,104},{48,112},{56,120},{... | collective-permute-start | bytes 442376 | tf_op jit(solution)/shard_map/ppermute | solution.py:19
  240.2 14.2 %copy-start.61 = (f32[32]{0:T(128)S(1)}, f32[32]{0:T(128)}, u32[]{:S(2)}) copy-start(f32[32]{0:T(128)} %multiply_power_fusion) | copy-start | bytes 388
  240.2 14.2 %copy-start.63 = (f32[128]{0:T(128)S(1)}, f32[128]{0:T(128)}, u32[]{:S(2)}) copy-start(f32[128]{0:T(128)} %get-tuple-element.10) | copy-start | bytes 1540
  240.3 14.2 %copy-start.64 = (f32[128]{0:T(128)S(1)}, f32[128]{0:T(128)}, u32[]{:S(2)}) copy-start(f32[128]{0:T(128)} %get-tuple-element.81) | copy-start | bytes 1540
  240.3 14.2 %copy-start.65 = (f32[128]{0:T(128)S(1)}, f32[128]{0:T(128)}, u32[]{:S(2)}) copy-start(f32[128]{0:T(128)} %get-tuple-element.82) | copy-start | bytes 1540
  240.3 14.2 %copy-start.76 = (f32[128]{0:T(128)S(1)}, f32[128]{0:T(128)}, u32[]{:S(2)}) copy-start(f32[128]{0:T(128)} %add_convert_fusion.9) | copy-start | bytes 1540
  240.4 12.6 %collective-permute-start.6 = (bf16[128,576]{0,1:T(8,128)(2,1)S(1)}, bf16[128,576]{0,1:T(8,128)(2,1)S(1)}, u32[]{:S(2)}, u32[]{:S(2)}) collective-permute-start(bf16[128,576]{0,1:T(8,128)(2,1)S(1)} %collective-permute-done.5), channel_id=1, source_target_pairs={{0,64},{8,72},{16,80},{24,88},{32,96},{40,104},{48,112},{56,120},{... | collective-permute-start | bytes 442376 | tf_op jit(solution)/shard_map/ppermute | solution.py:19
  273.0 3.5 copy-start.31
  290.4 7.5 copy-start.58
  290.4 8.5 copy-start.23
  290.4 8.7 copy-start.30
  290.4 60.4 %copy-start.20 = (bf16[128,1536]{1,0:T(8,128)(2,1)S(1)}, bf16[128,1536]{1,0:T(8,128)(2,1)}, u32[]{:S(2)}) copy-start(bf16[128,1536]{1,0:T(8,128)(2,1)} %param.12) | copy-start | bytes 1179652
  290.4 605.5 %copy-start.1 = (bf16[512,2048]{1,0:T(8,128)(2,1)S(1)}, bf16[512,2048]{1,0:T(8,128)(2,1)}, u32[]{:S(2)}) copy-start(bf16[512,2048]{1,0:T(8,128)(2,1)} %param.15) | copy-start | bytes 6291460
  (41 other events, 68.4 us)
Sparse Core Ops, SparseCore 0:
  15.9 122.1 all-gather.2
  352.8 536.8 all-reduce.4
where the time goes:
time: 905 us; the launch traced here: 903 us
  waiting for transfers between devices  592 us (65%)
  blocking collectives  131 us (14%)
  local copies, waits for them, and re-layouts  66.2 us (7%)
  matrix products  47 us (5%)
  other arithmetic  30 us (3%)
  starting transfers between devices  20.1 us (2%)
  between operations  16.3 us (2%)
    psum x1, waiting for transfers between devices, body(): grad_qb, grad_qa = lax.psum((qb_term, qa_term), 'ctx')  535 us
    all_gather x1, blocking collectives, body(): all_offsets = lax.all_gather(block_starts, 'ctx', axis=0, tiled=True)  80.7 us
    ppermute x7, waiting for transfers between devices, passed_along(): return lax.ppermute(value, axis, pairs)  56.6 us
    psum x1, blocking collectives, body(): lax.psum(columns_contract(query_gradient, query_adapter_second), 'head')  50.8 us
    unnamed x181, local copies, waits for them, and re-layouts  26.2 us
    ppermute x7, starting transfers between devices, passed_along(): return lax.ppermute(value, axis, pairs)  20 us
  transfers between devices with their start and end apart: 9, of which 7 were waited for; matrix products, arithmetic and copies ran while one was open for 12% of the time, Pallas kernels for 0%

commit v1 on v0

v1 whole, which is shorter than its diff:
```python
import functools

import jax
import jax.numpy as jnp
from jax import lax
from jax.experimental import pallas as pl
from jax.experimental.pallas import tpu as pltpu
from jax.sharding import PartitionSpec as P

PLAIN_WIDTH = 128
ROTARY_WIDTH = 64
VALUE_WIDTH = 128
KVL = 512
SPAN = 8
ROPE_BASE = 10000.0
MESH = pl.DeviceIdType.MESH
VMEM = pltpu.VMEM
DMA = pltpu.SemaphoreType.DMA


def rotate(vectors, positions, sign):
    half_width = vectors.shape[-1] // 2
    freq = ROPE_BASE ** (-jnp.arange(half_width, dtype=jnp.float32) * 2.0 / vectors.shape[-1])
    angle = positions.astype(jnp.float32)[..., None] * freq
    angle = angle.reshape(
        positions.shape + (1,) * (vectors.ndim - positions.ndim - 1) + (half_width,)
    )
    cosine = jnp.cos(angle)
    sine = jnp.sin(angle) * sign
    first = vectors[..., :half_width]
    second = vectors[..., half_width:]
    return jnp.concatenate([first * cosine - second * sine, second * cosine + first * sine], -1)


def block_positions(offsets, half_rows):
    steps = jnp.arange(half_rows, dtype=jnp.int32)
    return jnp.concatenate([offsets[..., :1] + steps, offsets[..., 1:] + steps], -1)


def contract_rows(left, right):
    return lax.dot_general(
        left, right, (((0,), (0,)), ((), ())), preferred_element_type=jnp.float32
    )


def columns_contract(left, right):
    return lax.dot_general(
        left, right, (((1,), (1,)), ((), ())), preferred_element_type=jnp.float32
    )


def send(src, dst, send_sem, recv_sem, axis, target):
    copy = pltpu.make_async_remote_copy(
        src_ref=src,
        dst_ref=dst,
        send_sem=send_sem,
        recv_sem=recv_sem,
        device_id={axis: target},
        device_id_type=MESH,
    )
    copy.start()
    return copy


def greet(axis, targets):
    barrier = pltpu.get_barrier_semaphore()
    for target in targets:
        pl.semaphore_signal(barrier, inc=1, device_id={axis: target}, device_id_type=MESH)
    pl.semaphore_wait(barrier, len(targets))


def places(place):
    core = lax.rem(place, 2)
    y = lax.rem(place // 2, 8)
    z = place // 16
    partner = place + 1 - 2 * core
    return core, y, z, partner


def gather_kernel(
    kv_ref, starts_ref, w_ref, cot_ref,
    kv_out, starts_out, w_out, cot_out,
    local_sem, kv_s, kv_r, st_s, st_r, pair_s, pair_r, z_s, z_r, y_s, y_r,
):
    place = lax.axis_index("ctx")
    core, y, z, partner = places(place)
    slot = place // 8
    kin = [lax.rem(place + 8 * step, 64) for step in range(1, SPAN)]
    up = z * 16 + lax.rem(y + 1, 8) * 2 + core
    down = z * 16 + lax.rem(y + 7, 8) * 2 + core
    greet("ctx", kin + [partner, up, down])

    own = [
        pltpu.make_async_copy(kv_ref, kv_out.at[slot], local_sem.at[0]),
        pltpu.make_async_copy(starts_ref, starts_out.at[slot], local_sem.at[1]),
        pltpu.make_async_copy(w_ref.at[core], w_out.at[z, y, core], local_sem.at[2]),
        pltpu.make_async_copy(cot_ref, cot_out.at[core], local_sem.at[3]),
    ]
    for copy in own:
        copy.start()
    pending = []
    swap_w = send(
        w_ref.at[1 - core], w_out.at[z, y, core], pair_s.at[0], pair_r.at[0], "ctx", partner
    )
    swap_cot = send(cot_ref, cot_out.at[core], pair_s.at[1], pair_r.at[1], "ctx", partner)
    line = []
    for step in range(1, 4):
        target = lax.rem(z + step, 4) * 16 + y * 2 + core
        line.append([
            send(
                w_ref.at[core], w_out.at[z, y, core],
                z_s.at[step - 1, 0], z_r.at[step - 1, 0], "ctx", target,
            )
        ])
    for step in range(1, SPAN):
        pending.append(
            send(starts_ref, starts_out.at[slot], st_s.at[step - 1], st_r.at[step - 1], "ctx", kin[step - 1])
        )
        pending.append(
            send(kv_ref, kv_out.at[slot], kv_s.at[step - 1], kv_r.at[step - 1], "ctx", kin[step - 1])
        )
    swap_w.wait_recv()
    for step in range(1, 4):
        target = lax.rem(z + step, 4) * 16 + y * 2 + core
        line[step - 1].append(
            send(
                w_out.at[z, y, 1 - core], w_out.at[z, y, 1 - core],
                z_s.at[step - 1, 1], z_r.at[step - 1, 1], "ctx", target,
            )
        )
    own[2].wait()
    rings = {}
    for step in range(1, 5):
        for unit in range(4):
            depth = lax.rem(z - unit + 4, 4)
            if step == 1:
                if unit:
                    line[unit - 1][0].wait_recv()
                    line[unit - 1][1].wait_recv()
            for side, target in ((0, up), (1, down)):
                if step > 1:
                    rings[side, step - 1, unit].wait_recv()
                if step == 4 and (unit // 2) != side:
                    continue
                shift = -(step - 1) if side == 0 else step - 1
                column = lax.rem(y + shift + 8, 8)
                rings[side, step, unit] = send(
                    w_out.at[depth, column], w_out.at[depth, column],
                    y_s.at[side, step - 1, unit], y_r.at[side, step - 1, unit], "ctx", target,
                )
    for unit in range(4):
        rings[unit // 2, 4, unit].wait_recv()
    for copy in pending + [swap_cot]:
        copy.wait_recv()
    for copy in pending + [swap_w, swap_cot] + line[0] + line[1] + line[2] + list(rings.values()):
        copy.wait_send()
    own[0].wait()
    own[1].wait()
    own[3].wait()


def swap_kernel(half_ref, out_ref, local_sem, send_sem, recv_sem):
    place = lax.axis_index("ctx")
    core, _, _, partner = places(place)
    greet("ctx", [partner])
    own = pltpu.make_async_copy(half_ref.at[core], out_ref.at[core], local_sem)
    own.start()
    copy = send(half_ref.at[1 - core], out_ref.at[core], send_sem, recv_sem, "ctx", partner)
    copy.wait()
    own.wait()


def head_kernel(part_ref, out_ref, landed, mine, s1, r1, s2, r2):
    place = lax.axis_index("head")
    peers = [lax.rem(place + step, 8) for step in range(1, 8)]
    greet("head", peers)
    copies = [
        send(part_ref.at[peer], landed.at[step], s1.at[step], r1.at[step], "head", peer)
        for step, peer in enumerate(peers)
    ]
    total = part_ref[place]
    for step, copy in enumerate(copies):
        copy.wait_recv()
        total = total + landed[step]
    rounded = total.astype(jnp.bfloat16)
    mine[...] = rounded
    out_ref[place] = rounded
    second = [
        send(mine, out_ref.at[place], s2.at[step], r2.at[step], "head", peer)
        for step, peer in enumerate(peers)
    ]
    for copy in second:
        copy.wait_recv()
    for copy in copies + second:
        copy.wait_send()


def reduce_kernel(
    x_ref, full_ref, tail_ref,
    r1, t1, r2, t2, r3, g0, ga, gy, sems_s, sems_r, local_sem,
):
    place = lax.axis_index("ctx")
    core, y, _, partner = places(place)
    row = lax.rem(y, 4)
    slot = place // 8
    kin = [lax.rem(slot + step, 8) for step in range(1, 8)]
    near = [lax.rem(row + step, 4) for step in range(1, 4)]
    kin_at = [8 * other + lax.rem(place, 8) for other in kin]
    near_at = [8 * slot + 2 * other + core for other in near]
    greet("ctx", kin_at + near_at + [partner])
    sent = []

    def go(index, src, dst, target):
        copy = send(src, dst, sems_s.at[index], sems_r.at[index], "ctx", target)
        sent.append(copy)
        return copy

    go(0, x_ref.at[1 - core], r1, partner).wait_recv()
    t1[...] = (x_ref[core].astype(jnp.float32) + r1[...].astype(jnp.float32)).astype(jnp.bfloat16)
    copies = [go(1 + i, t1.at[near[i]], r2.at[i], near_at[i]) for i in range(3)]
    total = x_ref[core, row].astype(jnp.float32) + r1[row].astype(jnp.float32)
    for i, copy in enumerate(copies):
        copy.wait_recv()
        total = total + r2[i].astype(jnp.float32)
    t2[...] = total.astype(jnp.bfloat16)
    copies = [go(4 + i, t2.at[kin[i]], r3.at[i], kin_at[i]) for i in range(7)]
    total = t2[slot].astype(jnp.float32)
    for i, copy in enumerate(copies):
        copy.wait_recv()
        total = total + r3[i].astype(jnp.float32)
    tail_ref[...] = total[16:]
    lead = total[:16].astype(jnp.bfloat16)
    g0[...] = lead
    ga[slot] = lead
    copies = [go(11 + i, g0, ga.at[slot], kin_at[i]) for i in range(7)]
    for copy in copies:
        copy.wait_recv()
    own = pltpu.make_async_copy(ga, gy.at[row], local_sem.at[0])
    own.start()
    copies = [go(18 + i, ga, gy.at[row], near_at[i]) for i in range(3)]
    for copy in copies:
        copy.wait_recv()
    own.wait()
    last = pltpu.make_async_copy(gy, full_ref.at[core], local_sem.at[1])
    last.start()
    go(21, gy, full_ref.at[core], partner).wait_recv()
    last.wait()
    for copy in sent:
        copy.wait_send()


def call(kernel, out_shape, scratch, ident, *operands):
    count = len(operands)
    specs = [pl.BlockSpec(memory_space=VMEM)]
    outs = jax.tree.map(lambda _: pl.BlockSpec(memory_space=VMEM), out_shape)
    return pl.pallas_call(
        kernel,
        out_shape=out_shape,
        in_specs=specs * count,
        out_specs=outs,
        scratch_shapes=scratch,
        compiler_params=pltpu.CompilerParams(
            collective_id=ident, has_side_effects=True, vmem_limit_bytes=48 * 1024 * 1024
        ),
    )(*operands)


def shaped(shape, dtype=jnp.bfloat16):
    return jax.ShapeDtypeStruct(shape, dtype)


def body(
    frozen_queries,
    query_latent_rows,
    key_value_latent,
    block_starts,
    latent_up_weight,
    query_adapter_first,
    query_adapter_second,
    output_adapter_first,
    output_adapter_second,
    frozen_output_weight,
    output_cotangent,
):
    token_rows = frozen_queries.shape[0]
    half_rows = token_rows // 2
    per_head_width = PLAIN_WIDTH + ROTARY_WIDTH
    head_number = query_adapter_second.shape[1] // per_head_width
    score_scale = per_head_width ** (-0.5)
    width = output_cotangent.shape[1]
    held_rows, held_columns = frozen_output_weight.shape
    half_out = held_rows // 2
    core = lax.rem(lax.axis_index("ctx"), 2)
    own_positions = block_positions(block_starts[0], half_rows)

    rope_key = rotate(key_value_latent[:, KVL:].astype(jnp.float32), own_positions, 1.0)
    kv_sent = jnp.concatenate([key_value_latent[:, :KVL], rope_key.astype(jnp.bfloat16)], -1)
    starts_sent = jnp.pad(block_starts, ((0, 7), (0, 126)))
    w_sent = frozen_output_weight.T.reshape(held_columns, 2, half_out).transpose(1, 0, 2)
    kv_all, starts_all, w_all, cot_pair = call(
        gather_kernel,
        (
            shaped((SPAN,) + kv_sent.shape),
            shaped((SPAN, 8, 128), jnp.int32),
            shaped((4, 8, 2, held_columns, half_out)),
            shaped((2,) + output_cotangent.shape),
        ),
        [
            DMA((4,)), DMA((7,)), DMA((7,)), DMA((7,)), DMA((7,)), DMA((2,)), DMA((2,)),
            DMA((3, 2)), DMA((3, 2)), DMA((2, 4, 4)), DMA((2, 4, 4)),
        ],
        0,
        kv_sent, starts_sent, w_sent, output_cotangent,
    )
    key_count = SPAN * token_rows
    kv_all = kv_all.reshape(key_count, KVL + ROTARY_WIDTH)
    key_positions = block_positions(starts_all[:, 0, :2], half_rows).reshape(key_count)

    cot_both = cot_pair.reshape(2 * token_rows, width)
    rank_both = columns_contract(cot_both, output_adapter_second).astype(jnp.bfloat16)
    adapter_half = lax.dynamic_slice_in_dim(output_adapter_first, core * half_out, half_out, 0)
    d_half = jnp.dot(cot_both, w_all.reshape(width, half_out), preferred_element_type=jnp.float32)
    d_half = (d_half + columns_contract(rank_both, adapter_half)).astype(jnp.bfloat16)
    d_both = call(
        swap_kernel, shaped((2, token_rows, half_out)), [DMA, DMA, DMA], 1,
        d_half.reshape(2, token_rows, half_out),
    )
    attended_gradient = d_both.reshape(2, token_rows, head_number // 2, VALUE_WIDTH)
    attended_gradient = attended_gradient.transpose(0, 2, 1, 3).reshape(
        head_number, token_rows, VALUE_WIDTH
    )
    output_rank_gradient = columns_contract(output_cotangent, output_adapter_second).astype(
        jnp.bfloat16
    )

    query_rank_rows = jnp.dot(
        query_latent_rows, query_adapter_first, preferred_element_type=jnp.float32
    ).astype(jnp.bfloat16)
    query_full = frozen_queries.astype(jnp.float32) + jnp.dot(
        query_rank_rows, query_adapter_second, preferred_element_type=jnp.float32
    )
    query_full = query_full.reshape(token_rows, head_number, per_head_width)
    query_full = jnp.concatenate(
        [query_full[..., :PLAIN_WIDTH], rotate(query_full[..., PLAIN_WIDTH:], own_positions, 1.0)],
        -1,
    ).astype(jnp.bfloat16)

    kv_up = jnp.dot(
        kv_all[:, :KVL], latent_up_weight, preferred_element_type=jnp.float32
    ).astype(jnp.bfloat16)
    rope_keys = kv_all[:, KVL:]
    kv_heads = kv_up.reshape(key_count, head_number, PLAIN_WIDTH + VALUE_WIDTH)
    key_nope = kv_heads[..., :PLAIN_WIDTH]
    values = kv_heads[..., PLAIN_WIDTH:]
    scores = jnp.einsum(
        "qhd,khd->hqk", query_full[..., :PLAIN_WIDTH], key_nope, preferred_element_type=jnp.float32
    ) + jnp.einsum(
        "qhd,kd->hqk", query_full[..., PLAIN_WIDTH:], rope_keys, preferred_element_type=jnp.float32
    )
    causal = key_positions[None, :] <= own_positions[:, None]
    scores = jnp.where(causal[None], scores * score_scale, -jnp.inf)
    top = jnp.max(scores, -1, keepdims=True)
    expo = jnp.exp(scores - top)
    weights = (expo / jnp.sum(expo, -1, keepdims=True)).astype(jnp.bfloat16)
    attended = jnp.einsum(
        "hqk,khv->qhv", weights, values, preferred_element_type=jnp.float32
    ).astype(jnp.bfloat16)
    attended = attended.reshape(token_rows, head_number * VALUE_WIDTH)
    d_prob = jnp.einsum(
        "hqv,khv->hqk", attended_gradient, values, preferred_element_type=jnp.float32
    )
    weights_wide = weights.astype(jnp.float32)
    delta = jnp.sum(weights_wide * d_prob, -1, keepdims=True)
    d_score = (weights_wide * (d_prob - delta) * score_scale).astype(jnp.bfloat16)
    dq_nope = jnp.einsum("hqk,khd->qhd", d_score, key_nope, preferred_element_type=jnp.float32)
    dq_rope = jnp.einsum("hqk,kd->qhd", d_score, rope_keys, preferred_element_type=jnp.float32)
    dq_rope = rotate(dq_rope, own_positions, -1.0)
    query_gradient = (
        jnp.concatenate([dq_nope, dq_rope], -1)
        .reshape(token_rows, head_number * per_head_width)
        .astype(jnp.bfloat16)
    )

    rank = query_adapter_first.shape[1]
    o_part = jnp.dot(attended, output_adapter_first, preferred_element_type=jnp.float32)
    q_part = columns_contract(query_gradient, query_adapter_second)
    part = jnp.concatenate([o_part, q_part, jnp.zeros((token_rows, 128 - 2 * rank), jnp.float32)], -1)
    rows = token_rows // 8
    low = call(
        head_kernel, shaped((8, rows, 128)),
        [
            VMEM((7, rows, 128), jnp.float32), VMEM((rows, 128), jnp.bfloat16),
            DMA((7,)), DMA((7,)), DMA((7,)), DMA((7,)),
        ],
        2, part.reshape(8, rows, 128),
    ).reshape(token_rows, 128)
    output_rank_rows = low[:, :rank]
    query_adapter_gradient = low[:, rank:2 * rank]

    qb_term = contract_rows(query_rank_rows, query_gradient)
    oa_term = contract_rows(output_rank_gradient, attended)
    qa_term = contract_rows(query_adapter_gradient, query_latent_rows)
    ob_term = contract_rows(output_rank_rows, output_cotangent)
    ob_term = ob_term.astype(jnp.bfloat16).reshape(rank, 8, 4, 2, held_columns)
    ob_term = ob_term.transpose(3, 2, 1, 0, 4).reshape(64, -1, 128)
    lead = [term.astype(jnp.bfloat16).reshape(64, -1, 128) for term in (qb_term, oa_term, qa_term)]
    sizes = [term.shape[1] for term in lead]
    pieces = jnp.concatenate(lead + [ob_term], 1)
    pieces = jnp.pad(pieces, ((0, 0), (0, 32 - pieces.shape[1]), (0, 0)))
    bf = jnp.bfloat16
    full, tail = call(
        reduce_kernel,
        (shaped((2, 4, 8, 16, 128)), shaped((16, 128), jnp.float32)),
        [
            VMEM((4, 8, 32, 128), bf), VMEM((4, 8, 32, 128), bf), VMEM((3, 8, 32, 128), bf),
            VMEM((8, 32, 128), bf), VMEM((7, 32, 128), bf), VMEM((16, 128), bf),
            VMEM((8, 16, 128), bf), VMEM((4, 8, 16, 128), bf), DMA((22,)), DMA((22,)), DMA((2,)),
        ],
        3, pieces.reshape(2, 4, 8, 32, 128),
    )
    full = full.reshape(64, 16, 128).astype(jnp.float32)
    first, second = sizes[0], sizes[0] + sizes[1]
    grad_qb = full[:, :first].reshape(qb_term.shape)
    grad_oa = full[:, first:second].reshape(oa_term.shape).T
    grad_qa = full[:, second:].reshape(qa_term.shape).T
    grad_ob = tail[:ob_term.shape[1]].reshape(rank, held_columns)
    return (grad_qa, grad_qb, grad_oa, grad_ob)


def solution(mesh):
    return jax.shard_map(
        body,
        mesh=mesh,
        in_specs=(
            P("ctx", "head"),
            P("ctx", None),
            P("ctx", None),
            P("ctx", None),
            P(None, "head"),
            P(),
            P(None, "head"),
            P("head", None),
            P(),
            P("head", "ctx"),
            P("ctx", None),
        ),
        out_specs=(P(), P(None, "head"), P("head", None), P(None, "ctx")),
        check_vma=False,
    )
```

time: 905 us -> 211 us (0.23)
  waiting for transfers between devices: 592 us -> 0 us
  Pallas kernels: 0 us -> 131 us
  blocking collectives: 131 us -> 0 us
  local copies, waits for them, and re-layouts: 66.2 us -> 25.5 us
  other arithmetic: 30 us -> 9.77 us
  starting transfers between devices: 20.1 us -> 0 us
  between operations: 16.3 us -> 1.11 us
    psum x1 -> x0, waiting for transfers between devices: 535 us -> none  [body(): grad_qb, grad_qa = lax.psum((qb_term, qa_term), 'ctx')]
    pallas_call x0 -> x4, Pallas kernels: none -> 131 us  [call(): pl.pallas_call(kernel, out_shape=out_shape, in_specs=specs * count, out_s...]
    all_gather x1 -> x0, blocking collectives: 80.7 us -> none  [body(): all_offsets = lax.all_gather(block_starts, 'ctx', axis=0, tiled=True)]
    ppermute x7 -> x0, waiting for transfers between devices: 56.6 us -> none  [passed_along(): return lax.ppermute(value, axis, pairs)]
    psum x1 -> x0, blocking collectives: 50.8 us -> none  [body(): lax.psum(columns_contract(query_gradient, query_adapter_second), 'head')]
    ppermute x7 -> x0, starting transfers between devices: 20 us -> none  [passed_along(): return lax.ppermute(value, axis, pairs)]
    unnamed x181 -> x43, local copies, waits for them, and re-layouts: 26.2 us -> 7.15 us
    concatenate x10 -> x1, local copies, waits for them, and re-layouts: 14.7 us -> 0.61 us  [body(): jnp.concatenate([o_part, q_part, jnp.zeros((token_rows, 128 - 2 * rank),...]
  transfers between devices with their start and end apart: 9 -> 0, of which waited for: 7 -> 0; matrix products, arithmetic and copies ran while one was open for 12% -> 0% of each run, Pallas kernels for 0% -> 0%
where the time goes in v1:
time: 211 us; the launch traced here: 210 us
  Pallas kernels  131 us (62%)
  matrix products  42.9 us (20%)
  local copies, waits for them, and re-layouts  25.5 us (12%)
  other arithmetic  9.77 us (5%)
    pallas_call x4, Pallas kernels, call(): pl.pallas_call(kernel, out_shape=out_shape, in_specs=specs * count, out_s...  131 us
    unnamed x43, local copies, waits for them, and re-layouts  7.15 us
    dot_general x1, matrix products, body(): jnp.einsum('hqk,khd->qhd', d_score, key_nope, preferred_element_type=jnp....  6.9 us
    dot_general x1, matrix products, body(): jnp.einsum('hqk,kd->qhd', d_score, rope_keys, preferred_element_type=jnp....  6.72 us
    sub x1, matrix products, body(): expo = jnp.exp(scores - top)  5.86 us
    dot_general x1, matrix products, body(): jnp.einsum('hqv,khv->hqk', attended_gradient, values, preferred_element_t...  4.26 us

profile of v1, /device:TPU:1, one launch (start us, length us, event | category | flops | bytes accessed | tf_op | source)
XLA Modules:
  0.0 210.1 jit_solution(6430560017332732194)
XLA Ops:
  0.7 0.6 pad.16.clone
  1.3 1.3 fusion.60
  2.6 1.3 iota_add_fusion.2
  4.0 0.7 pad.8.starts_ref
  4.7 1.2 convolution_convert_fusion.7
  5.9 0.7 slice.94
  6.8 0.9 copy.100
  7.7 0.9 slice.93
  8.7 1.0 fusion.40
  9.7 1.5 copy.65
  11.2 0.9 copy.60
  12.1 0.7 copy.61
  12.8 0.9 pad_maximum_fusion.2.kv_ref
  13.7 2.1 convolution_add_fusion
  15.7 2.3 %copy.57 = f32[128,1536]{0,1:T(8,128)} copy(f32[128,1536]{1,0:T(8,128)} %convolution_add_fusion) | data formatting | bytes 1572864 | tf_op jit(solution)/shard_map/add | solution.py:339
  18.0 1.0 subtract_convert_fusion.1
  19.1 72.8 %shard_map.138 = (bf16[8,128,576]{2,1,0:T(8,128)(2,1)S(1)}, s32[8,8,128]{2,1,0:T(8,128)S(1)}, bf16[4,8,2,40,512]{4,3,2,1,0:T(8,128)(2,1)S(1)}, bf16[2,128,2560]{2,1,0:T(8,128)(2,1)S(1)}) custom-call(bf16[128,576]{1,0:T(8,128)(2,1)S(1)} %pad_maximum_fusion.2.kv_ref, s32[8,128]{1,0:T(8,128)S(1)} %pad.8.starts_ref, bf16[2,40,512]{2,1,0:T(8,128)(2,1)S(1)} %bitcast.89, ...), custom_call_target="tpu_custom_call" | custom-call | tf_op jit(solution)/shard_map/pallas_call | solution.py:256
  91.9 1.0 copy-done.2
  92.9 1.1 copy-done.3
  94.0 1.5 copy-done.4
  96.0 3.8 %fusion.64 = f32[256,512]{1,0:T(8,128)} fusion(bf16[256,2560]{1,0:T(8,128)(2,1)} %bitcast.86, bf16[2560,512]{1,0:T(8,128)(2,1)} %bitcast.97), kind=kOutput, calls=%fused_computation.97 | convolution fusion | flops 671088640 | bytes 4456448 | tf_op jit(solution)/shard_map/dot_general | solution.py:322
  99.8 2.3 %fusion.24 = bf16[256,512]{1,0:T(8,128)(2,1)S(1)} fusion(f32[256,512]{1,0:T(8,128)} %fusion.64, bf16[256,2560]{1,0:T(8,128)(2,1)} %bitcast.87, bf16[32,2560]{1,0:T(8,128)(2,1)S(1)} %copy-done.10, bf16[1024,32]{0,1:T(8,128)(2,1)S(1)} %copy-done.14, s32[]{:T(128)S(6)} %select_n.8), kind=kOutput, calls=%fused_computation.31 | convolution fusion | flops 50601984 | bytes 2293764 | tf_op jit(solution)/shard_map/dot_general | solution.py:47
  102.1 4.1 %shard_map.139 = bf16[2,128,512]{2,1,0:T(8,128)(2,1)S(1)} custom-call(bf16[2,128,512]{2,1,0:T(8,128)(2,1)S(1)} %bitcast.88), custom_call_target="tpu_custom_call" | custom-call | tf_op jit(solution)/shard_map/pallas_call | solution.py:256
  106.3 3.6 %convolution_convert_fusion = bf16[1024,2048]{1,0:T(8,128)(2,1)S(1)} fusion(bf16[512,2048]{1,0:T(8,128)(2,1)S(1)} %copy-done, bf16[1024,576]{1,0:T(8,128)(2,1)} %bitcast.93), kind=kOutput, calls=%fused_computation.11 | convolution fusion | flops 2149580800 | bytes 7340032 | tf_op jit(solution)/shard_map/dot_general | solution.py:348
  109.9 1.5 copy.82
  111.4 1.7 fusion.57
  113.0 1.3 copy-done.6
  114.4 2.7 %fusion.16 = f32[8,128,1024]{2,1,0:T(8,128)} fusion(bf16[1024,8,128]{2,1,0:T(8,128)(2,1)S(1)} %get-tuple-element.19, f32[128,8,192]{0,2,1:T(8,128)S(1)} %bitcast.103), kind=kOutput, calls=%fused_computation.26 | convolution fusion | flops 268435456 | bytes 6553600 | tf_op jit(solution)/shard_map/qhd,khd->hqk/dot_general | solution.py:355
  117.1 5.9 %fusion.61 = (f32[8,128]{1,0:T(8,128)S(1)}, f32[8,128,1024]{2,1,0:T(8,128)}) fusion(f32[8,128,1024]{2,1,0:T(8,128)} %fusion.16, pred[128,1024]{1,0:T(8,128)(4,1)S(1)} %broadcast_compare_fusion, bf16[1024,576]{1,0:T(8,128)(2,1)} %bitcast.94, bf16[128,8,32]{0,2,1:T(8,128)(2,1)S(1)} %get-tuple-element.21, bf16[128,8,32]{0,2,1:T(8,128)(2,1)S(1)} %get-tuple-element.20), kind=kOutput, calls=%fused_computation.96 | convolution fusion | flops 139723776 | bytes 8916992 | tf_op jit(solution)/shard_map/sub | solution.py:363
  122.9 2.9 %divide_convert_fusion = bf16[8,128,1024]{2,1,0:T(8,128)(2,1)S(1)} fusion(f32[8,128,1024]{2,1,0:T(8,128)} %get-tuple-element.42, f32[8,128]{1,0:T(8,128)S(1)} %get-tuple-element.41), kind=kLoop, calls=%fused_computation.9 | loop fusion | flops 2097152 | bytes 6295552 | tf_op jit(solution)/shard_map/convert_element_type | solution.py:364
  125.8 1.0 fusion.18
  127.2 0.9 fusion.65
  128.1 0.6 convolution_convert_fusion.4
  128.6 0.7 reshape.218
  129.3 4.3 %fusion.13 = f32[8,128,1024]{2,1,0:T(8,128)} fusion(bf16[8,128,128]{2,1,0:T(8,128)(2,1)S(1)} %bitcast.105, bf16[1024,8,128]{2,1,0:T(8,128)(2,1)} %get-tuple-element.18), kind=kOutput, calls=%fused_computation.23 | convolution fusion | flops 268435456 | bytes 6553600 | tf_op jit(solution)/shard_map/hqv,khv->hqk/dot_general | solution.py:369
  133.6 6.9 %fusion.26 = bf16[128,8,128]{0,2,1:T(8,128)(2,1)S(1)} fusion(bf16[8,128,1024]{2,1,0:T(8,128)(2,1)} %copy-done.8, f32[8,128,1024]{2,1,0:T(8,128)} %fusion.13, bf16[1024,8,128]{2,1,0:T(8,128)(2,1)} %copy-done.6), kind=kOutput, calls=%fused_computation.33 | convolution fusion | flops 275908608 | bytes 8650752 | tf_op jit(solution)/shard_map/hqk,khd->qhd/dot_general | solution.py:375
  140.5 6.7 %fusion.25 = f32[128,8,64]{0,2,1:T(8,128)} fusion(bf16[8,128,1024]{2,1,0:T(8,128)(2,1)} %copy-done.8, f32[8,128,1024]{2,1,0:T(8,128)} %fusion.13, bf16[1024,576]{1,0:T(8,128)(2,1)} %bitcast.95), kind=kOutput, calls=%fused_computation.32 | convolution fusion | flops 141559808 | bytes 13107200 | tf_op jit(solution)/shard_map/hqk,kd->qhd/dot_general | solution.py:376
  147.3 1.1 subtract_convert_fusion
  149.0 19.8 %shard_map.140 = bf16[8,16,128]{2,1,0:T(8,128)(2,1)S(1)} custom-call(f32[8,16,128]{2,1,0:T(8,128)S(1)} %bitcast.92), custom_call_target="tpu_custom_call" | custom-call | tf_op jit(solution)/shard_map/pallas_call | solution.py:256
  168.9 0.4 reshape.216
  169.9 0.9 reshape.222
  171.2 0.7 reshape.223
  171.9 1.1 fusion.36
  173.0 34.2 %shard_map.141 = (bf16[2,4,8,16,128]{4,3,2,1,0:T(8,128)(2,1)S(1)}, f32[16,128]{1,0:T(8,128)S(1)}) custom-call(bf16[2,4,8,32,128]{4,3,2,1,0:T(8,128)(2,1)S(1)} %bitcast.85), custom_call_target="tpu_custom_call" | custom-call | tf_op jit(solution)/shard_map/pallas_call | solution.py:256
  207.1 0.7 reshape.228
  207.9 0.7 reshape.227
  208.7 0.7 reshape.226
  209.4 0.7 reshape.225
  (62 shorter events, 3.1 us)
Async XLA Ops:
  0.6 105.7 %copy-start = (bf16[512,2048]{1,0:T(8,128)(2,1)S(1)}, bf16[512,2048]{1,0:T(8,128)(2,1)}, u32[]{:S(2)}) copy-start(bf16[512,2048]{1,0:T(8,128)(2,1)} %param.15) | copy-start | bytes 6291460
  0.6 13.0 %copy-start.11 = (bf16[128,1536]{1,0:T(8,128)(2,1)S(1)}, bf16[128,1536]{1,0:T(8,128)(2,1)}, u32[]{:S(2)}) copy-start(bf16[128,1536]{1,0:T(8,128)(2,1)} %param.11) | copy-start | bytes 1179652
  5.9 12.2 %copy-start.15 = (bf16[128,32]{0,1:T(8,128)(2,1)}, bf16[128,32]{0,1:T(8,128)(2,1)S(1)}, u32[]{:S(2)}) copy-start(bf16[128,32]{0,1:T(8,128)(2,1)S(1)} %convolution_convert_fusion.7) | copy-start | bytes 24580
  8.7 10.3 %copy-start.1 = (bf16[128,2560]{1,0:T(8,128)(2,1)S(1)}, bf16[128,2560]{1,0:T(8,128)(2,1)}, u32[]{:S(2)}) copy-start(bf16[128,2560]{1,0:T(8,128)(2,1)} %cot_ref.1) | copy-start | bytes 1966084
  13.7 4.4 %copy-start.18 = (f32[128,32]{0,1:T(8,128)S(1)}, f32[128,32]{0,1:T(8,128)}, u32[]{:S(2)}) copy-start(f32[128,32]{0,1:T(8,128)} %copy.61) | copy-start | bytes 49156
  91.8 1.1 copy-start.2
  92.9 1.1 copy-start.3
  94.0 1.5 copy-start.4
  96.0 3.8 %copy-start.10 = (bf16[32,2560]{1,0:T(8,128)(2,1)S(1)}, bf16[32,2560]{1,0:T(8,128)(2,1)}, u32[]{:S(2)}) copy-start(bf16[32,2560]{1,0:T(8,128)(2,1)} %param.19) | copy-start | bytes 491524
  96.0 3.8 %copy-start.14 = (bf16[1024,32]{0,1:T(8,128)(2,1)S(1)}, bf16[1024,32]{0,1:T(8,128)(2,1)}, u32[]{:S(2)}) copy-start(bf16[1024,32]{0,1:T(8,128)(2,1)} %param.18) | copy-start | bytes 196612
  111.4 3.0 %copy-start.7 = (f32[128,1536]{0,1:T(8,128)S(1)}, f32[128,1536]{0,1:T(8,128)}, u32[]{:S(2)}) copy-start(f32[128,1536]{0,1:T(8,128)} %copy.57) | copy-start | bytes 2359300
  113.0 1.3 copy-start.6
  122.9 2.9 %copy-start.5 = (bf16[1024,8,128]{2,1,0:T(8,128)(2,1)S(1)}, bf16[1024,8,128]{2,1,0:T(8,128)(2,1)}, u32[]{:S(2)}) copy-start(bf16[1024,8,128]{2,1,0:T(8,128)(2,1)} %get-tuple-element.18) | copy-start | bytes 6291460
  125.8 1.3 copy-start.8
  140.5 6.8 %copy-start.17 = (f32[128,32]{0,1:T(8,128)S(1)}, f32[128,32]{0,1:T(8,128)}, u32[]{:S(2)}) copy-start(f32[128,32]{0,1:T(8,128)} %copy.65) | copy-start | bytes 49156
  140.5 7.9 %copy-start.12 = (bf16[32,1536]{1,0:T(8,128)(2,1)S(1)}, bf16[32,1536]{1,0:T(8,128)(2,1)}, u32[]{:S(2)}) copy-start(bf16[32,1536]{1,0:T(8,128)(2,1)} %param.17) | copy-start | bytes 294916
  140.5 8.2 %copy-start.16 = (bf16[128,32]{0,1:T(8,128)(2,1)S(1)}, bf16[128,32]{0,1:T(8,128)(2,1)}, u32[]{:S(2)}) copy-start(bf16[128,32]{0,1:T(8,128)(2,1)} %copy-done.15) | copy-start | bytes 24580
  147.2 1.7 copy-start.13
  147.3 1.7 copy-start.19
  147.3 22.0 %copy-start.9 = (bf16[128,1536]{1,0:T(8,128)(2,1)S(1)}, bf16[128,1536]{1,0:T(8,128)(2,1)}, u32[]{:S(2)}) copy-start(bf16[128,1536]{1,0:T(8,128)(2,1)} %param.12) | copy-start | bytes 1179652

commit v2 on v1

v2 whole, which is shorter than its diff:
```python
import functools

import jax
import jax.numpy as jnp
from jax import lax
from jax.experimental import pallas as pl
from jax.experimental.pallas import tpu as pltpu
from jax.sharding import PartitionSpec as P

PLAIN_WIDTH = 128
ROTARY_WIDTH = 64
VALUE_WIDTH = 128
KVL = 512
SPAN = 8
ROPE_BASE = 10000.0
MESH = pl.DeviceIdType.MESH
VMEM = pltpu.VMEM
DMA = pltpu.SemaphoreType.DMA


def block_positions(offsets, half_rows):
    steps = jnp.arange(half_rows, dtype=jnp.int32)
    return jnp.concatenate([offsets[..., :1] + steps, offsets[..., 1:] + steps], -1)


def contract_rows(left, right):
    return lax.dot_general(
        left, right, (((0,), (0,)), ((), ())), preferred_element_type=jnp.float32
    )


def columns_contract(left, right):
    return lax.dot_general(
        left, right, (((1,), (1,)), ((), ())), preferred_element_type=jnp.float32
    )


def send(src, dst, send_sem, recv_sem, axis, target):
    copy = pltpu.make_async_remote_copy(
        src_ref=src,
        dst_ref=dst,
        send_sem=send_sem,
        recv_sem=recv_sem,
        device_id={axis: target},
        device_id_type=MESH,
    )
    copy.start()
    return copy


def greet(axis, targets):
    barrier = pltpu.get_barrier_semaphore()
    for target in targets:
        pl.semaphore_signal(barrier, inc=1, device_id={axis: target}, device_id_type=MESH)
    pl.semaphore_wait(barrier, len(targets))


def places(place):
    core = lax.rem(place, 2)
    y = lax.rem(place // 2, 8)
    z = place // 16
    partner = place + 1 - 2 * core
    return core, y, z, partner


def rows_contract(left, right):
    return lax.dot_general(
        left, right, (((0,), (0,)), ((), ())), preferred_element_type=jnp.float32
    )


def dot(left, right):
    return jnp.dot(left, right, preferred_element_type=jnp.float32)


def turned(vectors, cosine, sine):
    lane = lax.broadcasted_iota(jnp.int32, vectors.shape, 1)
    other = jnp.where(
        lax.rem(lane, 64) < 32, pltpu.roll(vectors, 96, 1), pltpu.roll(vectors, 32, 1)
    )
    return vectors * cosine + other * sine


def attend_kernel(
    kv_ref, places_ref, w_ref, cot_ref, fqn_ref, fqr_ref, own_pos_ref, cos_ref, sin_ref,
    ql_ref, qa_ref, qbn_ref, qbr_ref, oa_ref, ob_ref, up_ref,
    o_out, q_out, qbn_out, qbr_out, oat_out,
    kv_all, place_all, w_all, cot_all, d_mine, d_all,
    qn_s, qr_s, low_s, kcat_s, val_s, wt_s, att_s, gn_s, gr_s,
    local_sem, kv_s, kv_r, st_s, st_r, pair_s, pair_r, z_s, z_r, y_s, y_r, x_s, x_r, f_s, f_r,
):
    place = lax.axis_index("ctx")
    core, y, z, partner = places(place)
    slot = place // 8
    head = lax.axis_index("head")
    x, block = lax.rem(head, 4), (head // 4) * 4
    right, left = block + lax.rem(x + 1, 4), block + lax.rem(x + 3, 4)
    kin = [lax.rem(place + 8 * step, 64) for step in range(1, SPAN)]
    up = z * 16 + lax.rem(y + 1, 8) * 2 + core
    down = z * 16 + lax.rem(y + 7, 8) * 2 + core
    barrier = pltpu.get_barrier_semaphore()
    for target in kin + [partner, up, down]:
        pl.semaphore_signal(barrier, inc=1, device_id={"ctx": target}, device_id_type=MESH)
    for target in (right, left):
        pl.semaphore_signal(barrier, inc=1, device_id={"head": target}, device_id_type=MESH)
    pl.semaphore_wait(barrier, len(kin) + 5)

    own = [
        pltpu.make_async_copy(kv_ref.at[x], kv_all.at[slot, x], local_sem.at[0]),
        pltpu.make_async_copy(places_ref, place_all.at[slot], local_sem.at[1]),
        pltpu.make_async_copy(w_ref.at[core], w_all.at[z, y, core], local_sem.at[2]),
        pltpu.make_async_copy(cot_ref, cot_all.at[core], local_sem.at[3]),
    ]
    for copy in own:
        copy.start()
    pending = []
    swap_w = send(
        w_ref.at[1 - core], w_all.at[z, y, core], pair_s.at[0], pair_r.at[0], "ctx", partner
    )
    first = []
    for step in range(1, SPAN):
        i = step - 1
        first.append(send(kv_ref.at[x], kv_all.at[slot, x], kv_s.at[i], kv_r.at[i], "ctx", kin[i]))
    for i in range(SPAN - 1):
        pending.append(
            send(places_ref, place_all.at[slot], st_s.at[i], st_r.at[i], "ctx", kin[i])
        )
    swap_cot = send(cot_ref, cot_all.at[core], pair_s.at[1], pair_r.at[1], "ctx", partner)
    pending.append(swap_cot)
    across = [
        [
            send(kv_ref.at[x], kv_all.at[slot, x], x_s.at[side, 0], x_r.at[side, 0], "head", target)
        ]
        for side, target in ((0, right), (1, left))
    ]
    line = []
    for step in range(1, 4):
        target = lax.rem(z + step, 4) * 16 + y * 2 + core
        line.append([
            send(
                w_ref.at[core], w_all.at[z, y, core],
                z_s.at[step - 1, 0], z_r.at[step - 1, 0], "ctx", target,
            )
        ])

    low_s[...] = dot(ql_ref[...], qa_ref[...]).astype(jnp.bfloat16)
    qn_s[...] = (fqn_ref[...].astype(jnp.float32) + dot(low_s[...], qbn_ref[...])).astype(
        jnp.bfloat16
    )
    for pair in range(4):
        lanes = slice(128 * pair, 128 * pair + 128)
        vectors = fqr_ref[:, lanes].astype(jnp.float32) + dot(low_s[...], qbr_ref[:, lanes])
        qr_s[:, lanes] = turned(vectors, cos_ref[...], sin_ref[...]).astype(jnp.bfloat16)

    swap_w.wait_recv()
    for step in range(1, 4):
        target = lax.rem(z + step, 4) * 16 + y * 2 + core
        line[step - 1].append(
            send(
                w_all.at[z, y, 1 - core], w_all.at[z, y, 1 - core],
                z_s.at[step - 1, 1], z_r.at[step - 1, 1], "ctx", target,
            )
        )
    own[2].wait()
    rings = {}

    def ring(step, unit):
        depth = lax.rem(z - unit + 4, 4)
        if step == 1 and unit:
            line[unit - 1][0].wait_recv()
            line[unit - 1][1].wait_recv()
        for side, target in ((0, up), (1, down)):
            if step > 1 and (side, step - 1, unit) in rings:
                rings[side, step - 1, unit].wait_recv()
            if step == 5 or (step == 4 and (unit // 2) != side):
                continue
            shift = -(step - 1) if side == 0 else step - 1
            column = lax.rem(y + shift + 8, 8)
            rings[side, step, unit] = send(
                w_all.at[depth, column], w_all.at[depth, column],
                y_s.at[side, step - 1, unit], y_r.at[side, step - 1, unit], "ctx", target,
            )

    ring(1, 0)
    for i in range(SPAN - 1):
        first[i].wait_recv()
        source = lax.rem(slot + 7 - i, 8)
        for side, target in ((0, right), (1, left)):
            across[side].append(
                send(
                    kv_all.at[source, x], kv_all.at[source, x],
                    x_s.at[side, i + 1], x_r.at[side, i + 1], "head", target,
                )
            )
    for unit in range(1, 4):
        ring(1, unit)
    relays = []
    for i in range(SPAN):
        source = lax.rem(slot + 8 - i, 8)
        across[0][i].wait_recv()
        across[1][i].wait_recv()
        if i % 2 == 0:
            target, lane = right, lax.rem(x + 3, 4)
        else:
            target, lane = left, lax.rem(x + 1, 4)
        relays.append(
            send(
                kv_all.at[source, lane], kv_all.at[source, lane],
                f_s.at[i], f_r.at[i], "head", target,
            )
        )
    for unit in range(4):
        ring(2, unit)
    own[0].wait()
    own[1].wait()
    for copy in relays + pending[:SPAN - 1]:
        copy.wait_recv()

    positions = jnp.concatenate([place_all[i, 0:1, :] for i in range(SPAN)], 1)
    keys = positions.shape[1]
    visible = positions <= own_pos_ref[...]
    latents = kv_all[...].reshape(keys, 640)
    rope2 = latents[:, KVL:]
    scale = (PLAIN_WIDTH + ROTARY_WIDTH) ** (-0.5)
    lane_half = lax.broadcasted_iota(jnp.int32, (qr_s.shape[0], 128), 1) // 64

    def forward(number, total):
        kv = dot(latents[:, :KVL], up_ref[:, pl.ds(pl.multiple_of(number * 256, 256), 256)])
        kv = kv.astype(jnp.bfloat16)
        kcat_s[number, :, :128] = kv[:, :128]
        kcat_s[number, :, 128:] = rope2
        val_s[number] = kv[:, 128:]
        plain = qn_s[:, pl.ds(pl.multiple_of(number * 128, 128), 128)]
        turn = qr_s[:, pl.ds(pl.multiple_of((number // 2) * 128, 128), 128)].astype(jnp.float32)
        turn = jnp.where(lane_half == lax.rem(number, 2), turn, 0.0).astype(jnp.bfloat16)
        query = jnp.concatenate([plain, turn], 1)
        scores = columns_contract(query, kcat_s[number]) * scale
        scores = jnp.where(visible, scores, -jnp.inf)
        expo = jnp.exp(scores - jnp.max(scores, -1, keepdims=True))
        weights = (expo / jnp.sum(expo, -1, keepdims=True)).astype(jnp.bfloat16)
        wt_s[number] = weights
        attended = dot(weights, val_s[number]).astype(jnp.bfloat16)
        att_s[:, pl.ds(pl.multiple_of(number * 128, 128), 128)] = attended
        return total + dot(attended, oa_ref[pl.ds(pl.multiple_of(number * 128, 128), 128), :])

    total = jnp.zeros(o_out.shape, jnp.float32)
    for part in range(4):
        total = lax.fori_loop(2 * part, 2 * part + 2, forward, total)
        if part < 3:
            for unit in range(4):
                ring(part + 3, unit)
    o_out[...] = total
    swap_cot.wait_recv()
    own[3].wait()

    tokens, half_out = d_mine.shape[1], d_mine.shape[2]
    cot = cot_all[...].reshape(2 * tokens, cot_all.shape[2])
    rank = columns_contract(cot, ob_ref[...]).astype(jnp.bfloat16)
    d_half = dot(cot, w_all[...].reshape(cot.shape[1], half_out)) + columns_contract(
        rank, oa_ref[pl.ds(pl.multiple_of(core * half_out, half_out), half_out), :]
    )
    d_mine[...] = d_half.astype(jnp.bfloat16).reshape(d_mine.shape)
    swap_d = send(
        d_mine.at[1 - core], d_all.at[core], pair_s.at[2], pair_r.at[2], "ctx", partner
    )
    keep = pltpu.make_async_copy(d_mine.at[core], d_all.at[core], local_sem.at[4])
    keep.start()
    rank_own = columns_contract(cot_ref[...], ob_ref[...]).astype(jnp.bfloat16)
    oat_out[...] = rows_contract(rank_own, att_s[...]).astype(jnp.bfloat16)
    swap_d.wait_recv()
    keep.wait()

    def backward(pair, total):
        turns = []
        for even in range(2):
            number = 2 * pair + even
            lanes = pl.ds(pl.multiple_of(lax.rem(number, 4) * 128, 128), 128)
            d_prob = columns_contract(d_all[number // 4, :, lanes], val_s[number])
            weights = wt_s[number].astype(jnp.float32)
            delta = jnp.sum(weights * d_prob, -1, keepdims=True)
            d_score = (weights * (d_prob - delta) * scale).astype(jnp.bfloat16)
            grad = dot(d_score, kcat_s[number])
            plain = grad[:, :128].astype(jnp.bfloat16)
            at = pl.ds(pl.multiple_of(number * 128, 128), 128)
            gn_s[:, at] = plain
            total = total + columns_contract(plain, qbn_ref[:, at])
            turns.append(turned(grad[:, 128:], cos_ref[...], -sin_ref[...]))
        turn = jnp.where(lane_half == 0, turns[0], turns[1]).astype(jnp.bfloat16)
        at = pl.ds(pl.multiple_of(pair * 128, 128), 128)
        gr_s[:, at] = turn
        return total + columns_contract(turn, qbr_ref[:, at])

    q_out[...] = lax.fori_loop(0, 4, backward, jnp.zeros(q_out.shape, jnp.float32))
    qbn_out[...] = rows_contract(low_s[...], gn_s[...]).astype(jnp.bfloat16)
    qbr_out[...] = rows_contract(low_s[...], gr_s[...]).astype(jnp.bfloat16)

    done = first + pending + [swap_w, swap_d] + line[0] + line[1] + line[2]
    for copy in done + across[0] + across[1] + relays + list(rings.values()):
        copy.wait_send()


def head_kernel(part_ref, out_ref, landed, mine, s1, r1, s2, r2):
    place = lax.axis_index("head")
    peers = [lax.rem(place + step, 8) for step in range(1, 8)]
    greet("head", peers)
    copies = [
        send(part_ref.at[peer], landed.at[step], s1.at[step], r1.at[step], "head", peer)
        for step, peer in enumerate(peers)
    ]
    total = part_ref[place]
    for step, copy in enumerate(copies):
        copy.wait_recv()
        total = total + landed[step]
    rounded = total.astype(jnp.bfloat16)
    mine[...] = rounded
    out_ref[place] = rounded
    second = [
        send(mine, out_ref.at[place], s2.at[step], r2.at[step], "head", peer)
        for step, peer in enumerate(peers)
    ]
    for copy in second:
        copy.wait_recv()
    for copy in copies + second:
        copy.wait_send()


def reduce_kernel(
    x_ref, full_ref, tail_ref,
    r1, t1, r2, t2, r3, g0, ga, gy, sems_s, sems_r, local_sem,
):
    place = lax.axis_index("ctx")
    core, y, _, partner = places(place)
    row = lax.rem(y, 4)
    slot = place // 8
    kin = [lax.rem(slot + step, 8) for step in range(1, 8)]
    near = [lax.rem(row + step, 4) for step in range(1, 4)]
    kin_at = [8 * other + lax.rem(place, 8) for other in kin]
    near_at = [8 * slot + 2 * other + core for other in near]
    greet("ctx", kin_at + near_at + [partner])
    sent = []

    def go(index, src, dst, target):
        copy = send(src, dst, sems_s.at[index], sems_r.at[index], "ctx", target)
        sent.append(copy)
        return copy

    go(0, x_ref.at[1 - core], r1, partner).wait_recv()
    t1[...] = (x_ref[core].astype(jnp.float32) + r1[...].astype(jnp.float32)).astype(jnp.bfloat16)
    copies = [go(1 + i, t1.at[near[i]], r2.at[i], near_at[i]) for i in range(3)]
    total = x_ref[core, row].astype(jnp.float32) + r1[row].astype(jnp.float32)
    for i, copy in enumerate(copies):
        copy.wait_recv()
        total = total + r2[i].astype(jnp.float32)
    t2[...] = total.astype(jnp.bfloat16)
    copies = [go(4 + i, t2.at[kin[i]], r3.at[i], kin_at[i]) for i in range(7)]
    total = t2[slot].astype(jnp.float32)
    for i, copy in enumerate(copies):
        copy.wait_recv()
        total = total + r3[i].astype(jnp.float32)
    tail_ref[...] = total[16:]
    lead = total[:16].astype(jnp.bfloat16)
    g0[...] = lead
    ga[slot] = lead
    copies = [go(11 + i, g0, ga.at[slot], kin_at[i]) for i in range(7)]
    for copy in copies:
        copy.wait_recv()
    own = pltpu.make_async_copy(ga, gy.at[row], local_sem.at[0])
    own.start()
    copies = [go(18 + i, ga, gy.at[row], near_at[i]) for i in range(3)]
    for copy in copies:
        copy.wait_recv()
    own.wait()
    last = pltpu.make_async_copy(gy, full_ref.at[core], local_sem.at[1])
    last.start()
    go(21, gy, full_ref.at[core], partner).wait_recv()
    last.wait()
    for copy in sent:
        copy.wait_send()


def call(kernel, out_shape, scratch, ident, *operands):
    count = len(operands)
    specs = [pl.BlockSpec(memory_space=VMEM)]
    outs = jax.tree.map(lambda _: pl.BlockSpec(memory_space=VMEM), out_shape)
    return pl.pallas_call(
        kernel,
        out_shape=out_shape,
        in_specs=specs * count,
        out_specs=outs,
        scratch_shapes=scratch,
        compiler_params=pltpu.CompilerParams(
            collective_id=ident, has_side_effects=True, vmem_limit_bytes=48 * 1024 * 1024
        ),
    )(*operands)


def shaped(shape, dtype=jnp.bfloat16):
    return jax.ShapeDtypeStruct(shape, dtype)


def body(
    frozen_queries,
    query_latent_rows,
    key_value_latent,
    block_starts,
    latent_up_weight,
    query_adapter_first,
    query_adapter_second,
    output_adapter_first,
    output_adapter_second,
    frozen_output_weight,
    output_cotangent,
):
    token_rows = frozen_queries.shape[0]
    half_rows = token_rows // 2
    per_head_width = PLAIN_WIDTH + ROTARY_WIDTH
    head_number = query_adapter_second.shape[1] // per_head_width
    width = output_cotangent.shape[1]
    rank = query_adapter_first.shape[1]
    held_rows, held_columns = frozen_output_weight.shape
    half_out = held_rows // 2
    bf = jnp.bfloat16
    own_positions = block_positions(block_starts[0], half_rows)

    lane = jnp.arange(128, dtype=jnp.int32)
    freq = ROPE_BASE ** (-(lane % 32).astype(jnp.float32) * 2.0 / ROTARY_WIDTH)
    angle = own_positions.astype(jnp.float32)[:, None] * freq[None, :]
    cosine = jnp.cos(angle)
    sine = jnp.where(lane[None, :] % 64 < 32, -jnp.sin(angle), jnp.sin(angle))
    raw = key_value_latent[:, KVL:].astype(jnp.float32)
    other = jnp.concatenate([raw[:, 32:], raw[:, :32]], 1)
    rope_key = (
        jnp.concatenate([raw, raw], 1) * cosine + jnp.concatenate([other, other], 1) * sine
    ).astype(bf)
    kv_sent = jnp.concatenate([key_value_latent[:, :KVL], rope_key], -1)
    places_sent = jnp.broadcast_to(own_positions[None, :], (8, token_rows))
    w_sent = frozen_output_weight.T.reshape(held_columns, 2, half_out).transpose(1, 0, 2)

    def parted(array):
        split = array.reshape(array.shape[0], head_number, per_head_width)
        return (
            split[..., :PLAIN_WIDTH].reshape(array.shape[0], -1),
            split[..., PLAIN_WIDTH:].reshape(array.shape[0], -1),
        )

    fqn, fqr = parted(frozen_queries)
    qbn, qbr = parted(query_adapter_second)
    keys = SPAN * token_rows
    plain, turn = fqn.shape[1], fqr.shape[1]
    o_part, q_part, qbn_term, qbr_term, oa_term = call(
        attend_kernel,
        (
            shaped((token_rows, rank), jnp.float32),
            shaped((token_rows, rank), jnp.float32),
            shaped((rank, plain)),
            shaped((rank, turn)),
            shaped((rank, held_rows)),
        ),
        [
            VMEM((SPAN, 4, token_rows // 4, 640), bf), VMEM((SPAN, 8, 128), jnp.int32),
            VMEM((4, 8, 2, held_columns, half_out), bf), VMEM((2, token_rows, width), bf),
            VMEM((2, token_rows, half_out), bf), VMEM((2, token_rows, half_out), bf),
            VMEM((token_rows, plain), bf), VMEM((token_rows, turn), bf),
            VMEM((token_rows, rank), bf), VMEM((head_number, keys, 256), bf),
            VMEM((head_number, keys, 128), bf), VMEM((head_number, token_rows, keys), bf),
            VMEM((token_rows, held_rows), bf), VMEM((token_rows, plain), bf),
            VMEM((token_rows, turn), bf),
            DMA((5,)), DMA((7,)), DMA((7,)), DMA((7,)), DMA((7,)), DMA((3,)), DMA((3,)),
            DMA((3, 2)), DMA((3, 2)), DMA((2, 4, 4)), DMA((2, 4, 4)), DMA((2, 8)), DMA((2, 8)),
            DMA((8,)), DMA((8,)),
        ],
        0,
        kv_sent.reshape(4, token_rows // 4, 640), places_sent, w_sent, output_cotangent,
        fqn, fqr, own_positions[:, None], cosine, sine, query_latent_rows, query_adapter_first,
        qbn, qbr, output_adapter_first, output_adapter_second, latent_up_weight,
    )

    part = jnp.concatenate([o_part, q_part, jnp.zeros((token_rows, 128 - 2 * rank), jnp.float32)], -1)
    rows = token_rows // 8
    low = call(
        head_kernel, shaped((8, rows, 128)),
        [
            VMEM((7, rows, 128), jnp.float32), VMEM((rows, 128), jnp.bfloat16),
            DMA((7,)), DMA((7,)), DMA((7,)), DMA((7,)),
        ],
        2, part.reshape(8, rows, 128),
    ).reshape(token_rows, 128)
    output_rank_rows = low[:, :rank]
    query_adapter_gradient = low[:, rank:2 * rank]

    qa_term = contract_rows(query_adapter_gradient, query_latent_rows)
    ob_term = contract_rows(output_rank_rows, output_cotangent)
    ob_term = ob_term.astype(jnp.bfloat16).reshape(rank, 8, 4, 2, held_columns)
    ob_term = ob_term.transpose(3, 2, 1, 0, 4).reshape(64, -1, 128)
    lead = [term.astype(jnp.bfloat16).reshape(64, -1, 128) for term in (qbn_term, qbr_term, oa_term, qa_term)]
    sizes = [term.shape[1] for term in lead]
    pieces = jnp.concatenate(lead + [ob_term], 1)
    pieces = jnp.pad(pieces, ((0, 0), (0, 32 - pieces.shape[1]), (0, 0)))
    full, tail = call(
        reduce_kernel,
        (shaped((2, 4, 8, 16, 128)), shaped((16, 128), jnp.float32)),
        [
            VMEM((4, 8, 32, 128), bf), VMEM((4, 8, 32, 128), bf), VMEM((3, 8, 32, 128), bf),
            VMEM((8, 32, 128), bf), VMEM((7, 32, 128), bf), VMEM((16, 128), bf),
            VMEM((8, 16, 128), bf), VMEM((4, 8, 16, 128), bf), DMA((22,)), DMA((22,)), DMA((2,)),
        ],
        3, pieces.reshape(2, 4, 8, 32, 128),
    )
    full = full.reshape(64, 16, 128).astype(jnp.float32)
    ends = [sum(sizes[: i + 1]) for i in range(4)]
    grad_qb = jnp.concatenate(
        [
            full[:, :ends[0]].reshape(rank, head_number, PLAIN_WIDTH),
            full[:, ends[0]:ends[1]].reshape(rank, head_number, ROTARY_WIDTH),
        ],
        -1,
    ).reshape(rank, -1)
    grad_oa = full[:, ends[1]:ends[2]].reshape(oa_term.shape).T
    grad_qa = full[:, ends[2]:].reshape(qa_term.shape).T
    grad_ob = tail[:ob_term.shape[1]].reshape(rank, held_columns)
    return (grad_qa, grad_qb, grad_oa, grad_ob)


def solution(mesh):
    return jax.shard_map(
        body,
        mesh=mesh,
        in_specs=(
            P("ctx", "head"),
            P("ctx", None),
            P("ctx", None),
            P("ctx", None),
            P(None, "head"),
            P(),
            P(None, "head"),
            P("head", None),
            P(),
            P("head", "ctx"),
            P("ctx", None),
        ),
        out_specs=(P(), P(None, "head"), P("head", None), P(None, "ctx")),
        check_vma=False,
    )
```

time: 211 us -> 155 us (0.73)
  matrix products: 42.9 us -> 0.52 us
  Pallas kernels: 131 us -> 118 us
  other arithmetic: 9.77 us -> 2.55 us
  local copies, waits for them, and re-layouts: 25.5 us -> 32.3 us
    dot_general x12 -> x0, matrix products: 35.7 us -> none  [the longest x1 6.9 us: body(): jnp.einsum('hqk,khd->qhd', d_score, key_nope, preferred_element_type=jnp....]
    pallas_call x4 -> x3, Pallas kernels: 131 us -> 118 us  [call(): pl.pallas_call(kernel, out_shape=out_shape, in_specs=specs * count, out_s...]
    unnamed x43, local copies, waits for them, and re-layouts: 7.15 us -> 13.8 us
    sub x1 -> x0, matrix products: 5.86 us -> none  [body(): expo = jnp.exp(scores - top)]
    reshape x3 -> x8, local copies, waits for them, and re-layouts: 2.15 us -> 7.59 us  [the longest x2 2.4 us: parted(): split[..., PLAIN_WIDTH:].reshape(array.shape[0], -1)]
    convert_element_type x3 -> x2, other arithmetic: 2.93 us -> 0.08 us  [the longest x1 0.08 us: body(): angle = own_positions.astype(jnp.float32)[:, None] * freq[None, :]]
    add x2 -> x0, local copies, waits for them, and re-layouts: 2.29 us -> none  [the longest x1 2.29 us: body(): frozen_queries.astype(jnp.float32)]
where the time goes in v2:
time: 155 us; the launch traced here: 154 us
  Pallas kernels  118 us (76%)
  local copies, waits for them, and re-layouts  32.3 us (21%)
  other arithmetic  2.55 us (2%)
    pallas_call x3, Pallas kernels, call(): pl.pallas_call(kernel, out_shape=out_shape, in_specs=specs * count, out_s...  118 us
    unnamed x43, local copies, waits for them, and re-layouts  13.8 us

profile of v2, /device:TPU:1, one launch (start us, length us, event | category | flops | bytes accessed | tf_op | source)
XLA Modules:
  0.0 154.4 jit_solution(16006370571502955931)
XLA Ops:
  0.6 1.3 fusion.12
  1.9 1.3 iota_add_fusion
  3.2 0.1 fusion.9
  3.3 0.7 slice.55
  4.0 0.1 copy.34
  4.2 0.1 fusion.11
  4.3 1.0 negate_select_fusion
  5.3 0.1 copy.23
  5.4 0.9 slice.54
  6.3 0.8 copy.24
  7.2 0.7 copy.29.own_pos_ref
  7.9 1.5 copy.26
  9.4 0.7 slice.73
  10.1 1.8 %copy.33.fqn_ref = bf16[128,1024]{1,0:T(8,128)(2,1)} copy(bf16[128,1024]{0,1:T(8,128)(2,1)} %bitcast.47) | data formatting | bytes 524288 | tf_op jit(solution)/shard_map/reshape | solution.py:442
  11.9 0.7 slice.74
  12.5 1.7 %copy.28.fqr_ref = bf16[128,512]{1,0:T(8,128)(2,1)} copy(bf16[128,512]{0,1:T(8,128)(2,1)} %bitcast.48) | data formatting | bytes 262144 | tf_op jit(solution)/shard_map/reshape | solution.py:443
  14.2 1.0 reshape.133
  15.3 0.6 copy.42
  15.9 0.7 reshape.135.qbr_ref
  16.6 1.1 copy.30.qa_ref
  17.8 1.7 %copy.31.oa_ref = bf16[1024,32]{1,0:T(8,128)(2,1)} copy(bf16[1024,32]{0,1:T(8,128)(2,1)} %param.18) | data formatting | bytes 131072 | tf_op args[7]
  19.5 0.9 copy.41
  20.4 0.9 copy-done.3
  21.3 0.9 copy-done.4
  22.3 0.9 copy-done.5
  23.2 0.9 copy-done.6
  24.1 0.8 copy-done.7
  24.9 0.8 copy-done.8
  25.8 0.8 copy-done.9
  26.6 0.8 copy-done.10
  27.4 0.9 copy-done.11
  28.4 0.8 copy-done.12
  29.1 64.6 %shard_map.138 = (f32[128,32]{1,0:T(8,128)S(1)}, f32[128,32]{1,0:T(8,128)S(1)}, bf16[32,1024]{1,0:T(8,128)(2,1)S(1)}, bf16[32,512]{1,0:T(8,128)(2,1)S(1)}, bf16[32,1024]{1,0:T(8,128)(2,1)S(1)}) custom-call(bf16[4,32,640]{2,1,0:T(8,128)(2,1)S(1)} %bitcast.37, s32[8,128]{1,0:T(8,128)S(1)} %broadcast_in_dim.24.places_ref, bf16[2,40,512]{2,1,0:T(8,128)(2,1)S(1)} %bitcast.38, ...), custom_call_target="tpu_custom_call" | custom-call | tf_op jit(solution)/shard_map/pallas_call | solution.py:385
  93.9 0.1 maximum_maximum_fusion
  93.9 19.5 %shard_map.139 = bf16[8,16,128]{2,1,0:T(8,128)(2,1)S(1)} custom-call(f32[8,16,128]{2,1,0:T(8,128)S(1)} %bitcast.42), custom_call_target="tpu_custom_call" | custom-call | tf_op jit(solution)/shard_map/pallas_call | solution.py:385
  113.5 0.2 convolution_convert_fusion
  113.8 0.9 reshape.142
  114.7 0.3 copy.40
  115.0 0.7 reshape.143
  115.7 0.3 convolution_convert_fusion.1
  116.0 0.1 reshape.141
  116.3 0.8 concatenate.33
  117.2 33.9 %shard_map.140 = (bf16[2,4,8,16,128]{4,3,2,1,0:T(8,128)(2,1)S(1)}, f32[16,128]{1,0:T(8,128)S(1)}) custom-call(bf16[2,4,8,32,128]{4,3,2,1,0:T(8,128)(2,1)S(1)} %bitcast.36), custom_call_target="tpu_custom_call" | custom-call | tf_op jit(solution)/shard_map/pallas_call | solution.py:385
  151.3 0.1 reshape.147
  151.4 0.8 reshape.148
  152.3 0.7 reshape.145
  153.0 0.7 reshape.149
  153.7 0.7 reshape.150
  (46 shorter events, 0.5 us)
Async XLA Ops:
  7.2 13.2 %copy-start = (bf16[128,2560]{1,0:T(8,128)(2,1)S(1)}, bf16[128,2560]{1,0:T(8,128)(2,1)}, u32[]{:S(2)}) copy-start(bf16[128,2560]{1,0:T(8,128)(2,1)} %cot_ref.1) | copy-start | bytes 1966084
  7.2 13.2 %copy-start.1 = (bf16[512,2048]{1,0:T(8,128)(2,1)S(1)}, bf16[512,2048]{1,0:T(8,128)(2,1)}, u32[]{:S(2)}) copy-start(bf16[512,2048]{1,0:T(8,128)(2,1)} %up_ref.1) | copy-start | bytes 6291460
  7.2 13.2 %copy-start.2 = (bf16[128,1536]{1,0:T(8,128)(2,1)S(1)}, bf16[128,1536]{1,0:T(8,128)(2,1)}, u32[]{:S(2)}) copy-start(bf16[128,1536]{1,0:T(8,128)(2,1)} %ql_ref.1) | copy-start | bytes 1179652
  20.4 1.0 copy-start.3
  21.3 0.9 copy-start.4
  22.3 0.9 copy-start.5
  23.2 0.9 copy-start.6
  24.1 0.8 copy-start.7
  24.9 0.8 copy-start.8
  25.8 0.8 copy-start.9
  26.6 0.8 copy-start.10
  27.4 0.9 copy-start.11
  28.4 0.8 copy-start.12
  93.7 19.7 %copy-start.13 = (bf16[32,1024]{1,0:T(8,128)(2,1)}, bf16[32,1024]{1,0:T(8,128)(2,1)S(1)}, u32[]{:S(2)}) copy-start(bf16[32,1024]{1,0:T(8,128)(2,1)S(1)} %get-tuple-element.13) | copy-start | bytes 196612
  93.7 19.7 %copy-start.15 = (bf16[32,1024]{1,0:T(8,128)(2,1)}, bf16[32,1024]{1,0:T(8,128)(2,1)S(1)}, u32[]{:S(2)}) copy-start(bf16[32,1024]{1,0:T(8,128)(2,1)S(1)} %get-tuple-element.11) | copy-start | bytes 196612
  93.8 19.7 %copy-start.17 = (bf16[32,512]{1,0:T(8,128)(2,1)}, bf16[32,512]{1,0:T(8,128)(2,1)S(1)}, u32[]{:S(2)}) copy-start(bf16[32,512]{1,0:T(8,128)(2,1)S(1)} %get-tuple-element.12) | copy-start | bytes 98308
  113.5 2.7 %copy-start.14 = (bf16[32,1024]{1,0:T(8,128)(2,1)S(1)}, bf16[32,1024]{1,0:T(8,128)(2,1)}, u32[]{:S(2)}) copy-start(bf16[32,1024]{1,0:T(8,128)(2,1)} %copy-done.13) | copy-start | bytes 196612
  113.7 2.4 %copy-start.16 = (bf16[32,1024]{1,0:T(8,128)(2,1)S(1)}, bf16[32,1024]{1,0:T(8,128)(2,1)}, u32[]{:S(2)}) copy-start(bf16[32,1024]{1,0:T(8,128)(2,1)} %copy-done.15) | copy-start | bytes 196612
  113.7 2.5 %copy-start.18 = (bf16[32,512]{1,0:T(8,128)(2,1)S(1)}, bf16[32,512]{1,0:T(8,128)(2,1)}, u32[]{:S(2)}) copy-start(bf16[32,512]{1,0:T(8,128)(2,1)} %copy-done.17) | copy-start | bytes 98308

commit v3 on v2

v3 whole, which is shorter than its diff:
```python
import functools

import jax
import jax.numpy as jnp
from jax import lax
from jax.experimental import pallas as pl
from jax.experimental.pallas import tpu as pltpu
from jax.sharding import PartitionSpec as P

PLAIN_WIDTH = 128
ROTARY_WIDTH = 64
VALUE_WIDTH = 128
KVL = 512
SPAN = 8
ROPE_BASE = 10000.0
MESH = pl.DeviceIdType.MESH
VMEM = pltpu.VMEM
DMA = pltpu.SemaphoreType.DMA


def block_positions(offsets, half_rows):
    steps = jnp.arange(half_rows, dtype=jnp.int32)
    return jnp.concatenate([offsets[..., :1] + steps, offsets[..., 1:] + steps], -1)


def columns_contract(left, right):
    return lax.dot_general(
        left, right, (((1,), (1,)), ((), ())), preferred_element_type=jnp.float32
    )


def send(src, dst, send_sem, recv_sem, axis, target):
    copy = pltpu.make_async_remote_copy(
        src_ref=src,
        dst_ref=dst,
        send_sem=send_sem,
        recv_sem=recv_sem,
        device_id={axis: target},
        device_id_type=MESH,
    )
    copy.start()
    return copy


def places(place):
    core = lax.rem(place, 2)
    y = lax.rem(place // 2, 8)
    z = place // 16
    partner = place + 1 - 2 * core
    return core, y, z, partner


def dot(left, right):
    return jnp.dot(left, right, preferred_element_type=jnp.float32)


def turned(vectors, cosine, sine):
    lane = lax.broadcasted_iota(jnp.int32, vectors.shape, 1)
    other = jnp.where(
        lax.rem(lane, 64) < 32, pltpu.roll(vectors, 96, 1), pltpu.roll(vectors, 32, 1)
    )
    return vectors * cosine + other * sine


def tree_reduce(
    at, x, r1, t1, r2, t2, r3, g0, ga, gy, full, tail, send_sem, recv_sem, local_sem, sent
):
    core, row, slot, partner, near, near_at, kin, kin_at = at
    used, kept = x.shape[2], gy.shape[1]

    def go(index, src, dst, target):
        copy = send(src, dst, send_sem.at[index], recv_sem.at[index], "ctx", target)
        sent.append(copy)
        return copy

    copy = go(0, x.at[1 - core], r1, partner)
    yield
    copy.wait_recv()
    t1[...] = (x[core].astype(jnp.float32) + r1[...].astype(jnp.float32)).astype(jnp.bfloat16)
    copies = [go(1 + i, t1.at[near[i]], r2.at[i], near_at[i]) for i in range(3)]
    yield
    total = x[core, row].astype(jnp.float32) + r1[row].astype(jnp.float32)
    for i, copy in enumerate(copies):
        copy.wait_recv()
        total = total + r2[i].astype(jnp.float32)
    total = total.astype(jnp.bfloat16)
    blank = jnp.zeros(total.shape[1:], jnp.bfloat16)
    for i in range(8):
        t2[i, 0] = total[i] if i < kept else blank
        if tail is not None:
            first = kept + 2 * (i // 3)
            t2[i, 1] = total[first]
            t2[i, 2] = total[first + 1]
    copies = [go(4 + i, t2.at[kin[i]], r3.at[i], kin_at[i]) for i in range(7)]
    yield
    total = t2[slot].astype(jnp.float32)
    for i, copy in enumerate(copies):
        copy.wait_recv()
        total = total + r3[i].astype(jnp.float32)
    if tail is not None:
        tail(total[1:3].reshape(32, 128))
    lead = total[0].astype(jnp.bfloat16)
    g0[...] = lead
    ga[slot] = lead
    copies = [go(11 + i, g0, ga.at[slot], kin_at[i]) for i in range(7)]
    yield
    for copy in copies:
        copy.wait_recv()
    own = pltpu.make_async_copy(ga.at[pl.ds(0, kept)], gy.at[row], local_sem.at[0])
    own.start()
    copies = [go(18 + i, ga.at[pl.ds(0, kept)], gy.at[row], near_at[i]) for i in range(3)]
    yield
    for copy in copies:
        copy.wait_recv()
    own.wait()
    last = pltpu.make_async_copy(gy, full.at[core], local_sem.at[1])
    last.start()
    copy = go(21, gy, full.at[core], partner)
    yield
    copy.wait_recv()
    last.wait()
    yield


def attend_kernel(
    kv_ref, places_ref, own_pos_ref, cos_ref, sin_ref,
    w_ref, cot_ref, fq_ref, ql_ref, qa_ref, qb_ref, oa_ref, ob_ref, up_ref,
    qa_out, qb_out, oa_out, ob_out,
    kv_all, place_all, w_all, cot_all, d_mine, d_all,
    fq_s, ql_s, qa_s, qb_s, oa_s, ob_s, up_s,
    qn_s, qr_s, kcat_s, val_s, wt_s, att_s, grad_s,
    part_s, hx_s, hy_s, hz_s,
    x1, r11, t11, r12, t12, r13, g10, ga1, gy1, full1,
    x2, r21, t21, r22, t22, r23, g20, ga2, gy2, full2,
    local_sem, kv_s, kv_r, st_s, st_r, pair_s, pair_r, z_s, z_r, y_s, y_r, x_s, x_r, f_s, f_r,
    h_s, h_r, tree_s, tree_r, tree_local,
):
    place = lax.axis_index("ctx")
    core, y, z, partner = places(place)
    slot = place // 8
    head = lax.axis_index("head")
    x, block = lax.rem(head, 4), (head // 4) * 4
    right, left = block + lax.rem(x + 1, 4), block + lax.rem(x + 3, 4)
    kin = [lax.rem(place + 8 * step, 64) for step in range(1, SPAN)]
    up = z * 16 + lax.rem(y + 1, 8) * 2 + core
    down = z * 16 + lax.rem(y + 7, 8) * 2 + core
    row = lax.rem(y, 4)
    kin_slot = [lax.rem(slot + step, 8) for step in range(1, 8)]
    near = [lax.rem(row + step, 4) for step in range(1, 4)]
    near_at = [8 * slot + 2 * other + core for other in near]
    beside = [block + lax.rem(x + step, 4) for step in range(1, 4)]
    facing = 4 - block + x
    barrier = pltpu.get_barrier_semaphore()
    for target in kin + near_at + [partner, up, down]:
        pl.semaphore_signal(barrier, inc=1, device_id={"ctx": target}, device_id_type=MESH)
    for target in beside + [facing]:
        pl.semaphore_signal(barrier, inc=1, device_id={"head": target}, device_id_type=MESH)
    pl.semaphore_wait(barrier, len(kin) + len(near_at) + 7)
    mine = pl.ds(pl.multiple_of(core * 512, 512), 512)
    theirs = pl.ds(pl.multiple_of((1 - core) * 512, 512), 512)

    own = [
        pltpu.make_async_copy(kv_ref.at[x], kv_all.at[slot, x], local_sem.at[0]),
        pltpu.make_async_copy(places_ref, place_all.at[slot], local_sem.at[1]),
        pltpu.make_async_copy(w_ref.at[:, mine], w_all.at[z, y, core], local_sem.at[2]),
        pltpu.make_async_copy(cot_ref, cot_all.at[core], local_sem.at[3]),
    ]
    for copy in own:
        copy.start()
    pending = []
    swap_w = send(
        w_ref.at[:, theirs], w_all.at[z, y, core], pair_s.at[0], pair_r.at[0], "ctx", partner
    )
    first = []
    for step in range(1, SPAN):
        i = step - 1
        first.append(send(kv_ref.at[x], kv_all.at[slot, x], kv_s.at[i], kv_r.at[i], "ctx", kin[i]))
    for i in range(SPAN - 1):
        pending.append(
            send(places_ref, place_all.at[slot], st_s.at[i], st_r.at[i], "ctx", kin[i])
        )
    swap_cot = send(cot_ref, cot_all.at[core], pair_s.at[1], pair_r.at[1], "ctx", partner)
    pending.append(swap_cot)
    across = [
        [
            send(kv_ref.at[x], kv_all.at[slot, x], x_s.at[side, 0], x_r.at[side, 0], "head", target)
        ]
        for side, target in ((0, right), (1, left))
    ]
    line = []
    for step in range(1, 4):
        target = lax.rem(z + step, 4) * 16 + y * 2 + core
        line.append([
            send(
                w_ref.at[:, mine], w_all.at[z, y, core],
                z_s.at[step - 1, 0], z_r.at[step - 1, 0], "ctx", target,
            )
        ])

    loads = [
        pltpu.make_async_copy(src, dst, local_sem.at[5 + i])
        for i, (src, dst) in enumerate((
            (ql_ref, ql_s), (qa_ref, qa_s), (fq_ref, fq_s), (qb_ref, qb_s), (up_ref, up_s),
            (oa_ref, oa_s), (ob_ref, ob_s),
        ))
    ]
    for copy in loads:
        copy.start()
    for copy in loads[:4]:
        copy.wait()
    low = columns_contract(ql_s[...], qa_s[...]).astype(jnp.bfloat16)
    low_turned = columns_contract(qa_s[...], ql_s[...]).astype(jnp.bfloat16)
    early = lax.broadcasted_iota(jnp.int32, (low.shape[0], 128), 1) < 64
    for pair in range(4):
        lanes = slice(384 * pair, 384 * pair + 384)
        vectors = fq_s[:, lanes].astype(jnp.float32) + dot(low, qb_s[:, lanes])
        one, two, three = [vectors[:, 128 * i:128 * i + 128] for i in range(3)]
        qn_s[:, 256 * pair:256 * pair + 128] = one.astype(jnp.bfloat16)
        qn_s[:, 256 * pair + 128:256 * pair + 256] = jnp.where(
            early, pltpu.roll(two, 64, 1), pltpu.roll(three, 64, 1)
        ).astype(jnp.bfloat16)
        qr_s[:, 128 * pair:128 * pair + 128] = turned(
            jnp.where(early, two, three), cos_ref[...], sin_ref[...]
        ).astype(jnp.bfloat16)

    swap_w.wait_recv()
    for step in range(1, 4):
        target = lax.rem(z + step, 4) * 16 + y * 2 + core
        line[step - 1].append(
            send(
                w_all.at[z, y, 1 - core], w_all.at[z, y, 1 - core],
                z_s.at[step - 1, 1], z_r.at[step - 1, 1], "ctx", target,
            )
        )
    own[2].wait()
    rings = {}

    def ring(step, unit):
        depth = lax.rem(z - unit + 4, 4)
        if step == 1 and unit:
            line[unit - 1][0].wait_recv()
            line[unit - 1][1].wait_recv()
        for side, target in ((0, up), (1, down)):
            if step > 1 and (side, step - 1, unit) in rings:
                rings[side, step - 1, unit].wait_recv()
            if step == 5 or (step == 4 and (unit // 2) != side):
                continue
            shift = -(step - 1) if side == 0 else step - 1
            column = lax.rem(y + shift + 8, 8)
            rings[side, step, unit] = send(
                w_all.at[depth, column], w_all.at[depth, column],
                y_s.at[side, step - 1, unit], y_r.at[side, step - 1, unit], "ctx", target,
            )

    ring(1, 0)
    for i in range(SPAN - 1):
        first[i].wait_recv()
        source = lax.rem(slot + 7 - i, 8)
        for side, target in ((0, right), (1, left)):
            across[side].append(
                send(
                    kv_all.at[source, x], kv_all.at[source, x],
                    x_s.at[side, i + 1], x_r.at[side, i + 1], "head", target,
                )
            )
    for unit in range(1, 4):
        ring(1, unit)
    relays = []
    for i in range(SPAN):
        source = lax.rem(slot + 8 - i, 8)
        across[0][i].wait_recv()
        across[1][i].wait_recv()
        if i % 2 == 0:
            target, lane = right, lax.rem(x + 3, 4)
        else:
            target, lane = left, lax.rem(x + 1, 4)
        relays.append(
            send(
                kv_all.at[source, lane], kv_all.at[source, lane],
                f_s.at[i], f_r.at[i], "head", target,
            )
        )
    for unit in range(4):
        ring(2, unit)
    own[0].wait()
    own[1].wait()
    for copy in relays + pending[:SPAN - 1]:
        copy.wait_recv()

    for copy in loads[4:]:
        copy.wait()
    positions = jnp.concatenate([place_all[i, 0:1, :] for i in range(SPAN)], 1)
    keys = positions.shape[1]
    visible = positions <= own_pos_ref[...]
    latents = kv_all[...].reshape(keys, 640)
    rope2 = latents[:, KVL:]
    scale = (PLAIN_WIDTH + ROTARY_WIDTH) ** (-0.5)
    lane_half = lax.broadcasted_iota(jnp.int32, (qr_s.shape[0], 128), 1) // 64

    def forward(number, total):
        kv = dot(latents[:, :KVL], up_s[:, pl.ds(pl.multiple_of(number * 256, 256), 256)])
        kv = kv.astype(jnp.bfloat16)
        kcat_s[number, :, :128] = kv[:, :128]
        kcat_s[number, :, 128:] = rope2
        val_s[number] = kv[:, 128:]
        plain = qn_s[:, pl.ds(pl.multiple_of(number * 128, 128), 128)]
        turn = qr_s[:, pl.ds(pl.multiple_of((number // 2) * 128, 128), 128)].astype(jnp.float32)
        turn = jnp.where(lane_half == lax.rem(number, 2), turn, 0.0).astype(jnp.bfloat16)
        query = jnp.concatenate([plain, turn], 1)
        scores = columns_contract(query, kcat_s[number]) * scale
        scores = jnp.where(visible, scores, -jnp.inf)
        expo = jnp.exp(scores - jnp.max(scores, -1, keepdims=True))
        weights = (expo / jnp.sum(expo, -1, keepdims=True)).astype(jnp.bfloat16)
        wt_s[number] = weights
        attended = dot(weights, val_s[number]).astype(jnp.bfloat16)
        att_s[:, pl.ds(pl.multiple_of(number * 128, 128), 128)] = attended
        return total + columns_contract(
            oa_s[:, pl.ds(pl.multiple_of(number * 128, 128), 128)], attended
        )

    total = jnp.zeros((32, 128), jnp.float32)
    for part in range(4):
        total = lax.fori_loop(2 * part, 2 * part + 2, forward, total)
        if part < 3:
            for unit in range(4):
                ring(part + 3, unit)
    part_s[:32] = total
    swap_cot.wait_recv()
    own[3].wait()

    tokens, half_out = d_mine.shape[1], d_mine.shape[2]
    cot = cot_all[...].reshape(2 * tokens, cot_all.shape[2])
    rank = columns_contract(cot, ob_s[...]).astype(jnp.bfloat16)
    d_half = dot(cot, w_all[...].reshape(cot.shape[1], half_out)) + dot(rank, oa_s[:, mine])
    d_mine[...] = d_half.astype(jnp.bfloat16).reshape(d_mine.shape)
    swap_d = send(
        d_mine.at[1 - core], d_all.at[core], pair_s.at[2], pair_r.at[2], "ctx", partner
    )
    keep = pltpu.make_async_copy(d_mine.at[core], d_all.at[core], local_sem.at[4])
    keep.start()
    rank_turned = columns_contract(ob_s[...], cot_all[core]).astype(jnp.bfloat16)
    oa_term = dot(rank_turned, att_s[...]).astype(jnp.bfloat16)
    for unit in range(24, 40):
        high, tile = (unit - 24) // 8, (unit - 24) % 8
        x1[unit // 20, unit // 5 % 4, unit % 5] = oa_term[
            16 * high:16 * high + 16, 128 * tile:128 * tile + 128
        ]
    swap_d.wait_recv()
    keep.wait()

    def backward(pair, total):
        turns, plains = [], []
        for even in range(2):
            number = 2 * pair + even
            lanes = pl.ds(pl.multiple_of(lax.rem(number, 4) * 128, 128), 128)
            d_prob = columns_contract(d_all[number // 4, :, lanes], val_s[number])
            weights = wt_s[number].astype(jnp.float32)
            delta = jnp.sum(weights * d_prob, -1, keepdims=True)
            d_score = (weights * (d_prob - delta) * scale).astype(jnp.bfloat16)
            grad = dot(d_score, kcat_s[number])
            plains.append(grad[:, :128])
            turns.append(turned(grad[:, 128:], cos_ref[...], -sin_ref[...]))
        turn = jnp.where(early, turns[0], turns[1])
        moved = pltpu.roll(plains[1], 64, 1)
        parts = [plains[0], jnp.where(early, turn, moved), jnp.where(early, moved, turn)]
        for i, piece in enumerate(parts):
            at = pl.ds(pl.multiple_of(pair * 384 + i * 128, 128), 128)
            piece = piece.astype(jnp.bfloat16)
            grad_s[:, at] = piece
            total = total + columns_contract(qb_s[:, at], piece)
        return total

    part_s[32:] = lax.fori_loop(0, 4, backward, jnp.zeros((32, 128), jnp.float32))
    heads = []
    for i in range(3):
        heads.append(send(part_s, hx_s.at[x], h_s.at[i], h_r.at[i], "head", beside[i]))
    hx_s[x] = part_s[...]
    qb_term = dot(low_turned, grad_s[...]).astype(jnp.bfloat16)
    for unit in range(24):
        high, tile = unit // 12, unit % 12
        x1[unit // 20, unit // 5 % 4, unit % 5] = qb_term[
            16 * high:16 * high + 16, 128 * tile:128 * tile + 128
        ]
    at = (core, row, slot, partner, near, near_at, kin_slot, kin)
    sent = []
    wide = tree_reduce(
        at, x1, r11, t11, r12, t12, r13, g10, ga1, gy1, full1, None,
        tree_s.at[0], tree_r.at[0], tree_local.at[0], sent,
    )
    next(wide)
    for copy in heads:
        copy.wait_recv()
    hy_s[...] = hx_s[0] + hx_s[1] + hx_s[2] + hx_s[3]
    heads.append(send(hy_s, hz_s, h_s.at[3], h_r.at[3], "head", facing))
    next(wide)
    heads[3].wait_recv()
    sums = (hy_s[...] + hz_s[...]).astype(jnp.bfloat16)
    qa_term = dot(sums[32:], ql_s[...]).astype(jnp.bfloat16)
    for unit in range(24):
        high, tile = unit // 12, unit % 12
        x2[unit // 12, unit // 3 % 4, unit % 3] = qa_term[
            16 * high:16 * high + 16, 128 * tile:128 * tile + 128
        ]
    ob_term = dot(sums[:32], cot_all[core])
    lane = lax.broadcasted_iota(jnp.int32, (32, 128), 1)

    def shifted(start, to):
        tile, offset = start // 128, start % 128
        shift = (to - offset) % 128
        value = pltpu.roll(ob_term[:, 128 * tile:128 * tile + 128], shift, 1)
        if offset + 40 > 128:
            after = pltpu.roll(ob_term[:, 128 * tile + 128:128 * tile + 256], shift, 1)
            value = jnp.where(lane < to + 128 - offset, value, after)
        return value

    for half in range(2):
        for line_row in range(4):
            for third in range(3):
                packed = jnp.zeros((32, 128), jnp.float32)
                for i in range(3):
                    member = 3 * third + i
                    if member > 7:
                        continue
                    value = shifted(40 * (8 * member + 2 * line_row + half), 40 * i)
                    inside = (lane >= 40 * i) & (lane < 40 * i + 40)
                    packed = jnp.where(inside, value, packed)
                packed = packed.astype(jnp.bfloat16)
                x2[half, line_row, 3 + 2 * third] = packed[:16]
                x2[half, line_row, 4 + 2 * third] = packed[16:]

    def tail(total):
        third = lax.rem(slot, 3)
        value = jnp.where(third == 1, pltpu.roll(total, 88, 1), total)
        value = jnp.where(third == 2, pltpu.roll(total, 48, 1), value)
        ob_out[...] = value[:, :40]

    slim = tree_reduce(
        at, x2, r21, t21, r22, t22, r23, g20, ga2, gy2, full2, tail,
        tree_s.at[1], tree_r.at[1], tree_local.at[1], sent,
    )
    for _ in range(5):
        next(slim)
        next(wide)
    for unit in range(40):
        value = full1[unit // 20, unit // 5 % 4, unit % 5].astype(jnp.float32)
        if unit < 24:
            high, tile, out = unit // 12, unit % 12, qb_out
        else:
            high, tile, out = (unit - 24) // 8, (unit - 24) % 8, oa_out
        out[16 * high:16 * high + 16, 128 * tile:128 * tile + 128] = value
    next(slim)
    next(slim)
    for unit in range(24):
        high, tile = unit // 12, unit % 12
        qa_out[16 * high:16 * high + 16, 128 * tile:128 * tile + 128] = full2[
            unit // 12, unit // 3 % 4, unit % 3
        ].astype(jnp.float32)

    done = first + pending + [swap_w, swap_d] + line[0] + line[1] + line[2] + heads + sent
    for copy in done + across[0] + across[1] + relays + list(rings.values()):
        copy.wait_send()


def shaped(shape, dtype=jnp.bfloat16):
    return jax.ShapeDtypeStruct(shape, dtype)


def body(
    frozen_queries,
    query_latent_rows,
    key_value_latent,
    block_starts,
    latent_up_weight,
    query_adapter_first,
    query_adapter_second,
    output_adapter_first,
    output_adapter_second,
    frozen_output_weight,
    output_cotangent,
):
    token_rows = frozen_queries.shape[0]
    half_rows = token_rows // 2
    per_head_width = PLAIN_WIDTH + ROTARY_WIDTH
    head_number = query_adapter_second.shape[1] // per_head_width
    width = output_cotangent.shape[1]
    rank = query_adapter_first.shape[1]
    held_rows, held_columns = frozen_output_weight.shape
    half_out = held_rows // 2
    bf = jnp.bfloat16
    own_positions = block_positions(block_starts[0], half_rows)

    lane = jnp.arange(128, dtype=jnp.int32)
    freq = ROPE_BASE ** (-(lane % 32).astype(jnp.float32) * 2.0 / ROTARY_WIDTH)
    angle = own_positions.astype(jnp.float32)[:, None] * freq[None, :]
    cosine = jnp.cos(angle)
    sine = jnp.where(lane[None, :] % 64 < 32, -jnp.sin(angle), jnp.sin(angle))
    raw = key_value_latent[:, KVL:].astype(jnp.float32)
    other = jnp.concatenate([raw[:, 32:], raw[:, :32]], 1)
    rope_key = (
        jnp.concatenate([raw, raw], 1) * cosine + jnp.concatenate([other, other], 1) * sine
    ).astype(bf)
    kv_sent = jnp.concatenate([key_value_latent[:, :KVL], rope_key], -1)
    places_sent = jnp.broadcast_to(own_positions[None, :], (8, token_rows))
    keys = SPAN * token_rows
    plain, turn = head_number * PLAIN_WIDTH, head_number * ROTARY_WIDTH

    def tree(used, kept, deep):
        return [
            VMEM((2, 4, used, 16, 128), bf), VMEM((4, used, 16, 128), bf),
            VMEM((4, used, 16, 128), bf), VMEM((3, used, 16, 128), bf),
            VMEM((8, deep, 16, 128), bf), VMEM((7, deep, 16, 128), bf), VMEM((16, 128), bf),
            VMEM((8, 16, 128), bf), VMEM((4, kept, 16, 128), bf), VMEM((2, 4, kept, 16, 128), bf),
        ]

    close, far = pl.BlockSpec(memory_space=VMEM), pl.BlockSpec(memory_space=pltpu.HBM)
    f32 = jnp.float32
    grad_qa, grad_qb, grad_oa, grad_ob = pl.pallas_call(
        attend_kernel,
        out_shape=(
            shaped((rank, query_latent_rows.shape[1]), f32),
            shaped(query_adapter_second.shape, f32),
            shaped((rank, held_rows), f32),
            shaped((rank, held_columns), f32),
        ),
        in_specs=[close] * 5 + [far] * 9,
        out_specs=(close,) * 4,
        scratch_shapes=[
            VMEM((SPAN, 4, token_rows // 4, 640), bf), VMEM((SPAN, 8, 128), jnp.int32),
            VMEM((4, 8, 2, held_columns, half_out), bf), VMEM((2, token_rows, width), bf),
            VMEM((2, token_rows, half_out), bf), VMEM((2, token_rows, half_out), bf),
            VMEM(frozen_queries.shape, bf), VMEM(query_latent_rows.shape, bf),
            VMEM((rank, query_latent_rows.shape[1]), bf), VMEM(query_adapter_second.shape, bf),
            VMEM((rank, held_rows), bf), VMEM((rank, width), bf), VMEM(latent_up_weight.shape, bf),
            VMEM((token_rows, plain), bf), VMEM((token_rows, turn), bf),
            VMEM((head_number, keys, 256), bf), VMEM((head_number, keys, 128), bf),
            VMEM((head_number, token_rows, keys), bf), VMEM((token_rows, held_rows), bf),
            VMEM(frozen_queries.shape, bf),
            VMEM((2 * rank, 128), f32), VMEM((4, 2 * rank, 128), f32),
            VMEM((2 * rank, 128), f32), VMEM((2 * rank, 128), f32),
            *tree(5, 5, 1), *tree(9, 3, 3),
            DMA((12,)), DMA((7,)), DMA((7,)), DMA((7,)), DMA((7,)), DMA((3,)), DMA((3,)),
            DMA((3, 2)), DMA((3, 2)), DMA((2, 4, 4)), DMA((2, 4, 4)), DMA((2, 8)), DMA((2, 8)),
            DMA((8,)), DMA((8,)), DMA((4,)), DMA((4,)), DMA((2, 22)), DMA((2, 22)), DMA((2, 2)),
        ],
        compiler_params=pltpu.CompilerParams(
            collective_id=0, has_side_effects=True, vmem_limit_bytes=56 * 1024 * 1024
        ),
    )(
        kv_sent.reshape(4, token_rows // 4, 640), places_sent, own_positions[:, None], cosine, sine,
        frozen_output_weight.T, output_cotangent, frozen_queries, query_latent_rows,
        query_adapter_first.T, query_adapter_second, output_adapter_first.T,
        output_adapter_second, latent_up_weight,
    )
    return (grad_qa.T, grad_qb, grad_oa.T, grad_ob)


def solution(mesh):
    return jax.shard_map(
        body,
        mesh=mesh,
        in_specs=(
            P("ctx", "head"),
            P("ctx", None),
            P("ctx", None),
            P("ctx", None),
            P(None, "head"),
            P(),
            P(None, "head"),
            P("head", None),
            P(),
            P("head", "ctx"),
            P("ctx", None),
        ),
        out_specs=(P(), P(None, "head"), P("head", None), P(None, "ctx")),
        check_vma=False,
    )
```

time: 155 us -> 121 us (0.78)
  local copies, waits for them, and re-layouts: 32.3 us -> 11.5 us
  Pallas kernels: 118 us -> 106 us
    pallas_call x3 -> x1, Pallas kernels: 118 us -> 106 us  [body(): pl.pallas_call(attend_kernel, out_shape=(shaped((rank, query_latent_rows....]
    reshape x17 -> x0, local copies, waits for them, and re-layouts: 11.3 us -> none  [the longest x2 2.4 us: parted(): split[..., PLAIN_WIDTH:].reshape(array.shape[0], -1)]
    unnamed x43 -> x5, local copies, waits for them, and re-layouts: 13.8 us -> 6.24 us
where the time goes in v3:
time: 121 us; the launch traced here: 120 us
  Pallas kernels  106 us (88%)
  local copies, waits for them, and re-layouts  11.5 us (10%)
  other arithmetic  2.39 us (2%)
    pallas_call x1, Pallas kernels, body(): pl.pallas_call(attend_kernel, out_shape=(shaped((rank, query_latent_rows....  106 us
    unnamed x5, local copies, waits for them, and re-layouts  6.24 us

profile of v3, /device:TPU:1, one launch (start us, length us, event | category | flops | bytes accessed | tf_op | source)
XLA Modules:
  0.0 120.3 jit_solution(13126869913868545485)
XLA Ops:
  0.7 1.3 %fusion.9 = (s32[1,1]{1,0:T(1,128)}, s32[1,1]{1,0:T(1,128)}) fusion(s32[1,2]{1,0:T(1,128)} %param.14), kind=kLoop, calls=%fused_computation.20 | loop fusion | bytes 16 | tf_op jit(solution)/shard_map/slice | solution.py:23
  2.0 1.3 %iota_add_fusion = (s32[64]{0:T(128)S(1)}, s32[64]{0:T(128)S(1)}) fusion(s32[]{:T(128)} %bitcast.1, s32[]{:T(128)} %bitcast), kind=kLoop, calls=%fused_computation.16 | loop fusion | flops 128 | bytes 520 | tf_op jit(solution)/shard_map/add | solution.py:23
  3.3 0.1 fusion.7
  3.3 0.6 broadcast_in_dim.13.places_ref
  3.9 0.7 slice.22
  4.7 0.1 copy.19
  4.8 0.7 copy.18.own_pos_ref
  5.5 0.1 fusion.8
  5.6 1.0 negate_select_fusion
  6.6 0.1 copy.16
  6.7 0.9 slice.21
  7.7 0.8 copy.17
  8.5 105.7 %shard_map.138 = (f32[32,1536]{1,0:T(8,128)}, f32[32,1536]{1,0:T(8,128)}, f32[32,1024]{1,0:T(8,128)}, f32[32,40]{1,0:T(8,128)}) custom-call(bf16[4,32,640]{2,1,0:T(8,128)(2,1)} %bitcast.9, s32[8,128]{1,0:T(8,128)} %broadcast_in_dim.13.places_ref, s32[128,1]{1,0:T(8,128)} %copy.18.own_pos_ref, f32[128,128]{1,0:T(8,128)} %get-tuple-element.18.cos_ref, ...), custom_call_target="tpu_custom_call" | custom-call | tf_op jit(solution)/shard_map/pallas_call | solution.py:517
  114.2 1.6 %copy.24 = f32[1536,32]{0,1:T(8,128)} copy(f32[1536,32]{0,1:T(8,128)} %bitcast.10) | data formatting | bytes 393216
  115.8 1.6 %copy.25 = f32[32,1536]{1,0:T(8,128)} copy(f32[32,1536]{1,0:T(8,128)} %get-tuple-element.28) | data formatting | bytes 393216
  117.4 1.6 %copy.26 = f32[1024,32]{0,1:T(8,128)} copy(f32[1024,32]{0,1:T(8,128)} %bitcast.11) | data formatting | bytes 262144
  119.0 1.3 %copy.27 = f32[32,40]{1,0:T(8,128)} copy(f32[32,40]{1,0:T(8,128)} %get-tuple-element.30) | data formatting | bytes 10240
  (4 shorter events, 0.0 us)

commit v4 on v3

--- a/solution.py
+++ b/solution.py
@@ -1,4 +1,4 @@
-import functools
+import math
 
 import jax
 import jax.numpy as jnp
@@ -18,11 +18,6 @@
 DMA = pltpu.SemaphoreType.DMA
 
 
-def block_positions(offsets, half_rows):
-    steps = jnp.arange(half_rows, dtype=jnp.int32)
-    return jnp.concatenate([offsets[..., :1] + steps, offsets[..., 1:] + steps], -1)
-
-
 def columns_contract(left, right):
     return lax.dot_general(
         left, right, (((1,), (1,)), ((), ())), preferred_element_type=jnp.float32
@@ -62,11 +57,9 @@
     return vectors * cosine + other * sine
 
 
-def tree_reduce(
-    at, x, r1, t1, r2, t2, r3, g0, ga, gy, full, tail, send_sem, recv_sem, local_sem, sent
-):
-    core, row, slot, partner, near, near_at, kin, kin_at = at
-    used, kept = x.shape[2], gy.shape[1]
+def tree_reduce(at, x, r1, t1, r2, t2, r3, g0, full, tail, send_sem, recv_sem, local_sem, sent):
+    core, row, slot, partner, near, near_at, kin, kin_at, group_at = at
+    kept = full.shape[2]
 
     def go(index, src, dst, target):
         copy = send(src, dst, send_sem.at[index], recv_sem.at[index], "ctx", target)
@@ -84,56 +77,44 @@
         copy.wait_recv()
         total = total + r2[i].astype(jnp.float32)
     total = total.astype(jnp.bfloat16)
-    blank = jnp.zeros(total.shape[1:], jnp.bfloat16)
     for i in range(8):
-        t2[i, 0] = total[i] if i < kept else blank
+        t2[i, :kept] = total[:kept]
         if tail is not None:
             first = kept + 2 * (i // 3)
-            t2[i, 1] = total[first]
-            t2[i, 2] = total[first + 1]
-    copies = [go(4 + i, t2.at[kin[i]], r3.at[i], kin_at[i]) for i in range(7)]
-    yield
-    total = t2[slot].astype(jnp.float32)
-    for i, copy in enumerate(copies):
-        copy.wait_recv()
-        total = total + r3[i].astype(jnp.float32)
-    if tail is not None:
-        tail(total[1:3].reshape(32, 128))
-    lead = total[0].astype(jnp.bfloat16)
-    g0[...] = lead
-    ga[slot] = lead
-    copies = [go(11 + i, g0, ga.at[slot], kin_at[i]) for i in range(7)]
+            t2[i, kept:] = total[first:first + 2]
+    copies = [go(4 + i, t2.at[kin[i]], r3.at[slot], kin_at[i]) for i in range(7)]
+    r3[slot] = t2[slot]
     yield
     for copy in copies:
         copy.wait_recv()
-    own = pltpu.make_async_copy(ga.at[pl.ds(0, kept)], gy.at[row], local_sem.at[0])
-    own.start()
-    copies = [go(18 + i, ga.at[pl.ds(0, kept)], gy.at[row], near_at[i]) for i in range(3)]
+    total = r3[0].astype(jnp.float32)
+    for i in range(1, 8):
+        total = total + r3[i].astype(jnp.float32)
+    if tail is not None:
+        tail(total[kept:].reshape(32, 128))
+    lead = total[:kept].astype(jnp.bfloat16)
+    g0[...] = lead
+    full[core, row] = lead
+    copies = [go(11 + i, g0, full.at[core, row], group_at[i]) for i in range(7)]
     yield
     for copy in copies:
         copy.wait_recv()
-    own.wait()
-    last = pltpu.make_async_copy(gy, full.at[core], local_sem.at[1])
-    last.start()
-    copy = go(21, gy, full.at[core], partner)
     yield
-    copy.wait_recv()
-    last.wait()
-    yield
 
 
 def attend_kernel(
-    kv_ref, places_ref, own_pos_ref, cos_ref, sin_ref,
+    starts_ref, kvt_ref,
     w_ref, cot_ref, fq_ref, ql_ref, qa_ref, qb_ref, oa_ref, ob_ref, up_ref,
-    qa_out, qb_out, oa_out, ob_out,
+    full_e, full_b, full_a, ob_out,
+    kvt_s, kv_pre, place_pre, kv_ref, places_ref, cos_ref, sin_ref,
     kv_all, place_all, w_all, cot_all, d_mine, d_all,
     fq_s, ql_s, qa_s, qb_s, oa_s, ob_s, up_s,
     qn_s, qr_s, kcat_s, val_s, wt_s, att_s, grad_s,
-    part_s, hx_s, hy_s, hz_s,
-    x1, r11, t11, r12, t12, r13, g10, ga1, gy1, full1,
-    x2, r21, t21, r22, t22, r23, g20, ga2, gy2, full2,
+    part_s, hx_s, hy_s, hz_s, po_s, ox_s, oy_s, oz_s,
+    xe, re1, te1, re2, te2, re3, ge, xb, rb1, tb1, rb2, tb2, rb3, gb,
+    xa, ra1, ta1, ra2, ta2, ra3, gq,
     local_sem, kv_s, kv_r, st_s, st_r, pair_s, pair_r, z_s, z_r, y_s, y_r, x_s, x_r, f_s, f_r,
-    h_s, h_r, tree_s, tree_r, tree_local,
+    h_s, h_r, tree_s, tree_r, load_sem,
 ):
     place = lax.axis_index("ctx")
     core, y, z, partner = places(place)
@@ -148,14 +129,51 @@
     kin_slot = [lax.rem(slot + step, 8) for step in range(1, 8)]
     near = [lax.rem(row + step, 4) for step in range(1, 4)]
     near_at = [8 * slot + 2 * other + core for other in near]
+    group_at = [8 * slot + lax.rem(lax.rem(place, 8) + step, 8) for step in range(1, 8)]
     beside = [block + lax.rem(x + step, 4) for step in range(1, 4)]
     facing = 4 - block + x
     barrier = pltpu.get_barrier_semaphore()
-    for target in kin + near_at + [partner, up, down]:
+    for target in kin + group_at + [up, down]:
         pl.semaphore_signal(barrier, inc=1, device_id={"ctx": target}, device_id_type=MESH)
     for target in beside + [facing]:
         pl.semaphore_signal(barrier, inc=1, device_id={"head": target}, device_id_type=MESH)
-    pl.semaphore_wait(barrier, len(kin) + len(near_at) + 7)
+    loads = [
+        pltpu.make_async_copy(src, dst, load_sem.at[i])
+        for i, (src, dst) in enumerate((
+            (kvt_ref, kvt_s), (ql_ref, ql_s), (qa_ref, qa_s), (fq_ref, fq_s), (qb_ref, qb_s),
+            (up_ref, up_s), (oa_ref, oa_s), (ob_ref, ob_s),
+        ))
+    ]
+    for copy in loads:
+        copy.start()
+    start, middle = starts_ref[0, 0], starts_ref[0, 1]
+
+    def spread(shape, axis):
+        step = lax.broadcasted_iota(jnp.int32, shape, axis)
+        return jnp.where(step < 64, step + start, step - 64 + middle)
+
+    lane = lax.broadcasted_iota(jnp.int32, (128, 128), 1)
+    power = lax.rem(lane, 32).astype(jnp.float32) * (-2.0 * math.log(ROPE_BASE) / ROTARY_WIDTH)
+    angle = spread((128, 128), 0).astype(jnp.float32) * jnp.exp(power)
+    cos_ref[...] = jnp.cos(angle)
+    sine = jnp.sin(angle)
+    sin_ref[...] = jnp.where(lax.rem(lane, 64) < 32, -sine, sine)
+    place_pre[...] = spread((8, 128), 1)
+    loads[0].wait()
+    raw = kvt_s[KVL:].astype(jnp.float32)
+    rope = turned(jnp.concatenate([raw, raw], 0).T, cos_ref[...], sin_ref[...])
+    latent = kvt_s[:KVL].astype(jnp.float32).T
+    kv_pre[:, :, :KVL] = latent.astype(jnp.bfloat16).reshape(4, 32, KVL)
+    kv_pre[:, :, KVL:] = rope.astype(jnp.bfloat16).reshape(4, 32, 128)
+    bounce = [
+        pltpu.make_async_copy(kv_pre, kv_ref, load_sem.at[8]),
+        pltpu.make_async_copy(place_pre, places_ref, load_sem.at[9]),
+    ]
+    for copy in bounce:
+        copy.start()
+    for copy in bounce:
+        copy.wait()
+    pl.semaphore_wait(barrier, len(kin) + len(group_at) + 6)
     mine = pl.ds(pl.multiple_of(core * 512, 512), 512)
     theirs = pl.ds(pl.multiple_of((1 - core) * 512, 512), 512)
 
@@ -197,16 +215,7 @@
             )
         ])
 
-    loads = [
-        pltpu.make_async_copy(src, dst, local_sem.at[5 + i])
-        for i, (src, dst) in enumerate((
-            (ql_ref, ql_s), (qa_ref, qa_s), (fq_ref, fq_s), (qb_ref, qb_s), (up_ref, up_s),
-            (oa_ref, oa_s), (ob_ref, ob_s),
-        ))
-    ]
-    for copy in loads:
-        copy.start()
-    for copy in loads[:4]:
+    for copy in loads[1:5]:
         copy.wait()
     low = columns_contract(ql_s[...], qa_s[...]).astype(jnp.bfloat16)
     low_turned = columns_contract(qa_s[...], ql_s[...]).astype(jnp.bfloat16)
@@ -287,11 +296,11 @@
     for copy in relays + pending[:SPAN - 1]:
         copy.wait_recv()
 
-    for copy in loads[4:]:
+    for copy in loads[5:]:
         copy.wait()
     positions = jnp.concatenate([place_all[i, 0:1, :] for i in range(SPAN)], 1)
     keys = positions.shape[1]
-    visible = positions <= own_pos_ref[...]
+    visible = positions <= spread((128, 1), 0)
     latents = kv_all[...].reshape(keys, 640)
     rope2 = latents[:, KVL:]
     scale = (PLAIN_WIDTH + ROTARY_WIDTH) ** (-0.5)
@@ -324,7 +333,9 @@
         if part < 3:
             for unit in range(4):
                 ring(part + 3, unit)
-    part_s[:32] = total
+    po_s[...] = total
+    ox_s[x] = total
+    heads = [send(po_s, ox_s.at[x], h_s.at[i], h_r.at[i], "head", beside[i]) for i in range(3)]
     swap_cot.wait_recv()
     own[3].wait()
 
@@ -340,13 +351,19 @@
     keep.start()
     rank_turned = columns_contract(ob_s[...], cot_all[core]).astype(jnp.bfloat16)
     oa_term = dot(rank_turned, att_s[...]).astype(jnp.bfloat16)
-    for unit in range(24, 40):
-        high, tile = (unit - 24) // 8, (unit - 24) % 8
-        x1[unit // 20, unit // 5 % 4, unit % 5] = oa_term[
+    for unit in range(16):
+        high, tile = unit // 8, unit % 8
+        xe[unit // 8, unit // 2 % 4, unit % 2] = oa_term[
             16 * high:16 * high + 16, 128 * tile:128 * tile + 128
         ]
+    for copy in heads:
+        copy.wait_recv()
+    oy_s[...] = ox_s[0] + ox_s[1] + ox_s[2] + ox_s[3]
+    heads.append(send(oy_s, oz_s, h_s.at[3], h_r.at[3], "head", facing))
     swap_d.wait_recv()
     keep.wait()
+    at = (core, row, slot, partner, near, near_at, kin_slot, kin, group_at)
+    sent = []
 
     def backward(pair, total):
         turns, plains = [], []
@@ -370,38 +387,10 @@
             total = total + columns_contract(qb_s[:, at], piece)
         return total
 
-    part_s[32:] = lax.fori_loop(0, 4, backward, jnp.zeros((32, 128), jnp.float32))
-    heads = []
-    for i in range(3):
-        heads.append(send(part_s, hx_s.at[x], h_s.at[i], h_r.at[i], "head", beside[i]))
-    hx_s[x] = part_s[...]
-    qb_term = dot(low_turned, grad_s[...]).astype(jnp.bfloat16)
-    for unit in range(24):
-        high, tile = unit // 12, unit % 12
-        x1[unit // 20, unit // 5 % 4, unit % 5] = qb_term[
-            16 * high:16 * high + 16, 128 * tile:128 * tile + 128
-        ]
-    at = (core, row, slot, partner, near, near_at, kin_slot, kin)
-    sent = []
-    wide = tree_reduce(
-        at, x1, r11, t11, r12, t12, r13, g10, ga1, gy1, full1, None,
-        tree_s.at[0], tree_r.at[0], tree_local.at[0], sent,
-    )
-    next(wide)
-    for copy in heads:
-        copy.wait_recv()
-    hy_s[...] = hx_s[0] + hx_s[1] + hx_s[2] + hx_s[3]
-    heads.append(send(hy_s, hz_s, h_s.at[3], h_r.at[3], "head", facing))
-    next(wide)
+    total = lax.fori_loop(0, 2, backward, jnp.zeros((32, 128), jnp.float32))
     heads[3].wait_recv()
-    sums = (hy_s[...] + hz_s[...]).astype(jnp.bfloat16)
-    qa_term = dot(sums[32:], ql_s[...]).astype(jnp.bfloat16)
-    for unit in range(24):
-        high, tile = unit // 12, unit % 12
-        x2[unit // 12, unit // 3 % 4, unit % 3] = qa_term[
-            16 * high:16 * high + 16, 128 * tile:128 * tile + 128
-        ]
-    ob_term = dot(sums[:32], cot_all[core])
+    o_low = (oy_s[...] + oz_s[...]).astype(jnp.bfloat16)
+    ob_term = dot(o_low, cot_all[core])
     lane = lax.broadcasted_iota(jnp.int32, (32, 128), 1)
 
     def shifted(start, to):
@@ -425,40 +414,81 @@
                     inside = (lane >= 40 * i) & (lane < 40 * i + 40)
                     packed = jnp.where(inside, value, packed)
                 packed = packed.astype(jnp.bfloat16)
-                x2[half, line_row, 3 + 2 * third] = packed[:16]
-                x2[half, line_row, 4 + 2 * third] = packed[16:]
+                xe[half, line_row, 2 + 2 * third] = packed[:16]
+                xe[half, line_row, 3 + 2 * third] = packed[16:]
 
     def tail(total):
         third = lax.rem(slot, 3)
         value = jnp.where(third == 1, pltpu.roll(total, 88, 1), total)
         value = jnp.where(third == 2, pltpu.roll(total, 48, 1), value)
-        ob_out[...] = value[:, :40]
-
+        ob_out[...] = value
+
+    soon = tree_reduce(
+        at, xe, re1, te1, re2, te2, re3, ge, full_e, tail,
+        tree_s.at[0], tree_r.at[0], None, sent,
+    )
+    next(soon)
+    total = lax.fori_loop(2, 3, backward, total)
+    next(soon)
+    total = lax.fori_loop(3, 4, backward, total)
+    part_s[...] = total
+    hx_s[x] = total
+    next(soon)
+    late = [send(part_s, hx_s.at[x], h_s.at[4 + i], h_r.at[4 + i], "head", beside[i]) for i in range(3)]
+    qb_term = dot(low_turned, grad_s[...]).astype(jnp.bfloat16)
+    for unit in range(24):
+        high, tile = unit // 12, unit % 12
+        xb[unit // 12, unit // 3 % 4, unit % 3] = qb_term[
+            16 * high:16 * high + 16, 128 * tile:128 * tile + 128
+        ]
+    wide = tree_reduce(
+        at, xb, rb1, tb1, rb2, tb2, rb3, gb, full_b, None,
+        tree_s.at[1], tree_r.at[1], None, sent,
+    )
+    next(wide)
+    for copy in late:
+        copy.wait_recv()
+    hy_s[...] = hx_s[0] + hx_s[1] + hx_s[2] + hx_s[3]
+    late.append(send(hy_s, hz_s, h_s.at[7], h_r.at[7], "head", facing))
+    next(wide)
+    next(soon)
+    late[3].wait_recv()
+    sums = (hy_s[...] + hz_s[...]).astype(jnp.bfloat16)
+    qa_term = dot(sums, ql_s[...]).astype(jnp.bfloat16)
+    for unit in range(24):
+        high, tile = unit // 12, unit % 12
+        xa[unit // 12, unit // 3 % 4, unit % 3] = qa_term[
+            16 * high:16 * high + 16, 128 * tile:128 * tile + 128
+        ]
     slim = tree_reduce(
-        at, x2, r21, t21, r22, t22, r23, g20, ga2, gy2, full2, tail,
-        tree_s.at[1], tree_r.at[1], tree_local.at[1], sent,
-    )
-    for _ in range(5):
-        next(slim)
-        next(wide)
-    for unit in range(40):
-        value = full1[unit // 20, unit // 5 % 4, unit % 5].astype(jnp.float32)
-        if unit < 24:
-            high, tile, out = unit // 12, unit % 12, qb_out
-        else:
-            high, tile, out = (unit - 24) // 8, (unit - 24) % 8, oa_out
-        out[16 * high:16 * high + 16, 128 * tile:128 * tile + 128] = value
+        at, xa, ra1, ta1, ra2, ta2, ra3, gq, full_a, None,
+        tree_s.at[2], tree_r.at[2], None, sent,
+    )
     next(slim)
     next(slim)
-    for unit in range(24):
-        high, tile = unit // 12, unit % 12
-        qa_out[16 * high:16 * high + 16, 128 * tile:128 * tile + 128] = full2[
-            unit // 12, unit // 3 % 4, unit % 3
-        ].astype(jnp.float32)
+    next(wide)
+    next(slim)
+    next(wide)
+    next(soon)
+    next(slim)
+    next(wide)
+    next(slim)
+    heads += late
 
     done = first + pending + [swap_w, swap_d] + line[0] + line[1] + line[2] + heads + sent
     for copy in done + across[0] + across[1] + relays + list(rings.values()):
         copy.wait_send()
+
+
+def finish_kernel(full_e, full_b, full_a, tail_ref, qa_out, qb_out, oa_out, ob_out):
+    for source, out, kept in ((full_a, qa_out, 3), (full_b, qb_out, 3), (full_e, oa_out, 2)):
+        tiles = out.shape[1] // 128
+        for unit in range(8 * kept):
+            high, tile = unit // tiles, unit % tiles
+            out[16 * high:16 * high + 16, 128 * tile:128 * tile + 128] = source[
+                unit // (4 * kept), unit // kept % 4, unit % kept
+            ].astype(jnp.float32)
+    ob_out[...] = tail_ref[...][:, :40]
 
 
 def shaped(shape, dtype=jnp.bfloat16):
@@ -479,7 +509,6 @@
     output_cotangent,
 ):
     token_rows = frozen_queries.shape[0]
-    half_rows = token_rows // 2
     per_head_width = PLAIN_WIDTH + ROTARY_WIDTH
     head_number = query_adapter_second.shape[1] // per_head_width
     width = output_cotangent.shape[1]
@@ -487,20 +516,6 @@
     held_rows, held_columns = frozen_output_weight.shape
     half_out = held_rows // 2
     bf = jnp.bfloat16
-    own_positions = block_positions(block_starts[0], half_rows)
-
-    lane = jnp.arange(128, dtype=jnp.int32)
-    freq = ROPE_BASE ** (-(lane % 32).astype(jnp.float32) * 2.0 / ROTARY_WIDTH)
-    angle = own_positions.astype(jnp.float32)[:, None] * freq[None, :]
-    cosine = jnp.cos(angle)
-    sine = jnp.where(lane[None, :] % 64 < 32, -jnp.sin(angle), jnp.sin(angle))
-    raw = key_value_latent[:, KVL:].astype(jnp.float32)
-    other = jnp.concatenate([raw[:, 32:], raw[:, :32]], 1)
-    rope_key = (
-        jnp.concatenate([raw, raw], 1) * cosine + jnp.concatenate([other, other], 1) * sine
-    ).astype(bf)
-    kv_sent = jnp.concatenate([key_value_latent[:, :KVL], rope_key], -1)
-    places_sent = jnp.broadcast_to(own_positions[None, :], (8, token_rows))
     keys = SPAN * token_rows
     plain, turn = head_number * PLAIN_WIDTH, head_number * ROTARY_WIDTH
 
@@ -508,23 +523,25 @@
         return [
             VMEM((2, 4, used, 16, 128), bf), VMEM((4, used, 16, 128), bf),
             VMEM((4, used, 16, 128), bf), VMEM((3, used, 16, 128), bf),
-            VMEM((8, deep, 16, 128), bf), VMEM((7, deep, 16, 128), bf), VMEM((16, 128), bf),
-            VMEM((8, 16, 128), bf), VMEM((4, kept, 16, 128), bf), VMEM((2, 4, kept, 16, 128), bf),
+            VMEM((8, deep, 16, 128), bf), VMEM((8, deep, 16, 128), bf), VMEM((kept, 16, 128), bf),
         ]
 
     close, far = pl.BlockSpec(memory_space=VMEM), pl.BlockSpec(memory_space=pltpu.HBM)
     f32 = jnp.float32
-    grad_qa, grad_qb, grad_oa, grad_ob = pl.pallas_call(
+    pieces = pl.pallas_call(
         attend_kernel,
         out_shape=(
-            shaped((rank, query_latent_rows.shape[1]), f32),
-            shaped(query_adapter_second.shape, f32),
-            shaped((rank, held_rows), f32),
-            shaped((rank, held_columns), f32),
+            shaped((2, 4, 2, 16, 128)),
+            shaped((2, 4, 3, 16, 128)),
+            shaped((2, 4, 3, 16, 128)),
+            shaped((rank, 128), f32),
         ),
-        in_specs=[close] * 5 + [far] * 9,
+        in_specs=[pl.BlockSpec(memory_space=pltpu.SMEM)] + [far] * 10,
         out_specs=(close,) * 4,
         scratch_shapes=[
+            VMEM((KVL + ROTARY_WIDTH, token_rows), bf), VMEM((4, token_rows // 4, 640), bf),
+            VMEM((8, 128), jnp.int32), VMEM((4, token_rows // 4, 640), bf),
+            VMEM((8, 128), jnp.int32), VMEM((128, 128), f32), VMEM((128, 128), f32),
             VMEM((SPAN, 4, token_rows // 4, 640), bf), VMEM((SPAN, 8, 128), jnp.int32),
             VMEM((4, 8, 2, held_columns, half_out), bf), VMEM((2, token_rows, width), bf),
             VMEM((2, token_rows, half_out), bf), VMEM((2, token_rows, half_out), bf),
@@ -535,22 +552,35 @@
             VMEM((head_number, keys, 256), bf), VMEM((head_number, keys, 128), bf),
             VMEM((head_number, token_rows, keys), bf), VMEM((token_rows, held_rows), bf),
             VMEM(frozen_queries.shape, bf),
-            VMEM((2 * rank, 128), f32), VMEM((4, 2 * rank, 128), f32),
-            VMEM((2 * rank, 128), f32), VMEM((2 * rank, 128), f32),
-            *tree(5, 5, 1), *tree(9, 3, 3),
-            DMA((12,)), DMA((7,)), DMA((7,)), DMA((7,)), DMA((7,)), DMA((3,)), DMA((3,)),
+            VMEM((rank, 128), f32), VMEM((4, rank, 128), f32),
+            VMEM((rank, 128), f32), VMEM((rank, 128), f32),
+            VMEM((rank, 128), f32), VMEM((4, rank, 128), f32),
+            VMEM((rank, 128), f32), VMEM((rank, 128), f32),
+            *tree(8, 2, 4), *tree(3, 3, 3), *tree(3, 3, 3),
+            DMA((5,)), DMA((7,)), DMA((7,)), DMA((7,)), DMA((7,)), DMA((3,)), DMA((3,)),
             DMA((3, 2)), DMA((3, 2)), DMA((2, 4, 4)), DMA((2, 4, 4)), DMA((2, 8)), DMA((2, 8)),
-            DMA((8,)), DMA((8,)), DMA((4,)), DMA((4,)), DMA((2, 22)), DMA((2, 22)), DMA((2, 2)),
+            DMA((8,)), DMA((8,)), DMA((8,)), DMA((8,)), DMA((3, 18)), DMA((3, 18)), DMA((10,)),
         ],
         compiler_params=pltpu.CompilerParams(
             collective_id=0, has_side_effects=True, vmem_limit_bytes=56 * 1024 * 1024
         ),
     )(
-        kv_sent.reshape(4, token_rows // 4, 640), places_sent, own_positions[:, None], cosine, sine,
+        block_starts, key_value_latent.T,
         frozen_output_weight.T, output_cotangent, frozen_queries, query_latent_rows,
         query_adapter_first.T, query_adapter_second, output_adapter_first.T,
         output_adapter_second, latent_up_weight,
     )
+    grad_qa, grad_qb, grad_oa, grad_ob = pl.pallas_call(
+        finish_kernel,
+        out_shape=(
+            shaped((rank, query_latent_rows.shape[1]), f32),
+            shaped(query_adapter_second.shape, f32),
+            shaped((rank, held_rows), f32),
+            shaped((rank, held_columns), f32),
+        ),
+        in_specs=[close] * 4,
+        out_specs=(close,) * 4,
+    )(*pieces)
     return (grad_qa.T, grad_qb, grad_oa.T, grad_ob)
 
 

time: 121 us -> 105 us (0.87)
  local copies, waits for them, and re-layouts: 11.5 us -> 0 us
  other arithmetic: 2.39 us -> 0 us
  Pallas kernels: 106 us -> 104 us
    unnamed x5 -> x0, local copies, waits for them, and re-layouts: 6.24 us -> none
    slice x4 -> x0, local copies, waits for them, and re-layouts: 3.04 us -> none  [the longest x1 1.31 us: block_positions(): offsets[..., :1] + steps]
    broadcast_in_dim x2 -> x0, local copies, waits for them, and re-layouts: 1.33 us -> none  [the longest x1 0.73 us: body(): own_positions[:, None]]
    add x1 -> x0, other arithmetic: 1.29 us -> none  [block_positions(): offsets[..., 1:] + steps]
    pallas_call x1 -> x2, Pallas kernels: 106 us -> 104 us  [the longest x1 103 us: body(): pl.pallas_call(attend_kernel, out_shape=(shaped((2, 4, 2, 16, 128)), shap...]
where the time goes in v4:
time: 105 us
  Pallas kernels  104 us (99%)
    pallas_call x1, Pallas kernels, body(): pl.pallas_call(attend_kernel, out_shape=(shaped((2, 4, 2, 16, 128)), shap...  103 us

profile of v4, /device:TPU:1, one launch (start us, length us, event | category | flops | bytes accessed | tf_op | source)
XLA Modules:
  0.0 105.1 jit_solution(4857277761279892713)
XLA Ops:
  0.6 102.7 %shard_map.138 = (bf16[2,4,2,16,128]{4,3,2,1,0:T(8,128)(2,1)}, bf16[2,4,3,16,128]{4,3,2,1,0:T(8,128)(2,1)}, bf16[2,4,3,16,128]{4,3,2,1,0:T(8,128)(2,1)}, f32[32,128]{1,0:T(8,128)}) custom-call(s32[1,2]{1,0:T(1,128)} %starts_ref.1, bf16[576,128]{1,0:T(8,128)(2,1)} %bitcast.6, bf16[40,1024]{1,0:T(8,128)(2,1)} %bitcast.8, bf16[128,2560]{1,0:T(8,128)(2,1)} %cot_ref.1, ...), custom_call_target="tpu_custom_call" | custom-call | tf_op jit(solution)/shard_map/pallas_call | solution.py:531
  103.3 1.8 %shard_map.139 = (f32[32,1536]{1,0:T(8,128)}, f32[32,1536]{1,0:T(8,128)}, f32[32,1024]{1,0:T(8,128)}, f32[32,40]{1,0:T(8,128)}) custom-call(bf16[2,4,2,16,128]{4,3,2,1,0:T(8,128)(2,1)} %get-tuple-element.12.full_e, bf16[2,4,3,16,128]{4,3,2,1,0:T(8,128)(2,1)} %get-tuple-element.13.full_b, bf16[2,4,3,16,128]{4,3,2,1,0:T(8,128)(2,1)} %get-tuple-element.14.full_a, ...), custom_call_target="tpu_custom_call" | custom-call | tf_op jit(solution)/shard_map/pallas_call | solution.py:573

commit v5 on v4

--- a/solution.py
+++ b/solution.py
@@ -289,8 +289,8 @@
                 f_s.at[i], f_r.at[i], "head", target,
             )
         )
-    for unit in range(4):
-        ring(2, unit)
+        if i % 2:
+            ring(2, i // 2)
     own[0].wait()
     own[1].wait()
     for copy in relays + pending[:SPAN - 1]:
@@ -319,7 +319,7 @@
         scores = columns_contract(query, kcat_s[number]) * scale
         scores = jnp.where(visible, scores, -jnp.inf)
         expo = jnp.exp(scores - jnp.max(scores, -1, keepdims=True))
-        weights = (expo / jnp.sum(expo, -1, keepdims=True)).astype(jnp.bfloat16)
+        weights = (expo * (1.0 / jnp.sum(expo, -1, keepdims=True))).astype(jnp.bfloat16)
         wt_s[number] = weights
         attended = dot(weights, val_s[number]).astype(jnp.bfloat16)
         att_s[:, pl.ds(pl.multiple_of(number * 128, 128), 128)] = attended
@@ -328,11 +328,17 @@
         )
 
     total = jnp.zeros((32, 128), jnp.float32)
-    for part in range(4):
-        total = lax.fori_loop(2 * part, 2 * part + 2, forward, total)
-        if part < 3:
-            for unit in range(4):
-                ring(part + 3, unit)
+    served = [
+        [(3, 0), (3, 1), (3, 2)], [(3, 3)], [(4, 0)], [(4, 1), (4, 2)], [(4, 3)], [], [],
+        [(5, 0), (5, 1), (5, 2), (5, 3)],
+    ]
+    done = 0
+    for number, turns in enumerate(served):
+        if turns:
+            total = lax.fori_loop(done, number + 1, forward, total)
+            done = number + 1
+        for step, unit in turns:
+            ring(step, unit)
     po_s[...] = total
     ox_s[x] = total
     heads = [send(po_s, ox_s.at[x], h_s.at[i], h_r.at[i], "head", beside[i]) for i in range(3)]
@@ -433,8 +439,10 @@
     total = lax.fori_loop(3, 4, backward, total)
     part_s[...] = total
     hx_s[x] = total
+    late = [
+        send(part_s, hx_s.at[x], h_s.at[4 + i], h_r.at[4 + i], "head", beside[i]) for i in range(3)
+    ]
     next(soon)
-    late = [send(part_s, hx_s.at[x], h_s.at[4 + i], h_r.at[4 + i], "head", beside[i]) for i in range(3)]
     qb_term = dot(low_turned, grad_s[...]).astype(jnp.bfloat16)
     for unit in range(24):
         high, tile = unit // 12, unit % 12

time: 105 us -> 102 us (0.971)
  Pallas kernels: 104 us -> 101 us
    pallas_call x1, Pallas kernels: 103 us -> 99.6 us  [body(): pl.pallas_call(attend_kernel, out_shape=(shaped((2, 4, 2, 16, 128)), shap...]
where the time goes in v5:
time: 102 us
  Pallas kernels  101 us (99%)
    pallas_call x1, Pallas kernels, body(): pl.pallas_call(attend_kernel, out_shape=(shaped((2, 4, 2, 16, 128)), shap...  99.6 us

profile of v5, /device:TPU:1, one launch (start us, length us, event | category | flops | bytes accessed | tf_op | source)
XLA Modules:
  0.0 102.0 jit_solution(12070665109967534948)
XLA Ops:
  0.6 99.6 %shard_map.138 = (bf16[2,4,2,16,128]{4,3,2,1,0:T(8,128)(2,1)}, bf16[2,4,3,16,128]{4,3,2,1,0:T(8,128)(2,1)}, bf16[2,4,3,16,128]{4,3,2,1,0:T(8,128)(2,1)}, f32[32,128]{1,0:T(8,128)}) custom-call(s32[1,2]{1,0:T(1,128)} %starts_ref.1, bf16[576,128]{1,0:T(8,128)(2,1)} %bitcast.6, bf16[40,1024]{1,0:T(8,128)(2,1)} %bitcast.8, bf16[128,2560]{1,0:T(8,128)(2,1)} %cot_ref.1, ...), custom_call_target="tpu_custom_call" | custom-call | tf_op jit(solution)/shard_map/pallas_call | solution.py:539
  100.2 1.8 %shard_map.139 = (f32[32,1536]{1,0:T(8,128)}, f32[32,1536]{1,0:T(8,128)}, f32[32,1024]{1,0:T(8,128)}, f32[32,40]{1,0:T(8,128)}) custom-call(bf16[2,4,2,16,128]{4,3,2,1,0:T(8,128)(2,1)} %get-tuple-element.12.full_e, bf16[2,4,3,16,128]{4,3,2,1,0:T(8,128)(2,1)} %get-tuple-element.13.full_b, bf16[2,4,3,16,128]{4,3,2,1,0:T(8,128)(2,1)} %get-tuple-element.14.full_a, ...), custom_call_target="tpu_custom_call" | custom-call | tf_op jit(solution)/shard_map/pallas_call | solution.py:581

commit v6 on v5

--- a/solution.py
+++ b/solution.py
@@ -262,7 +262,7 @@
             )
 
     ring(1, 0)
-    for i in range(SPAN - 1):
+    for i in (1, 3, 5, 0, 2, 4, 6):
         first[i].wait_recv()
         source = lax.rem(slot + 7 - i, 8)
         for side, target in ((0, right), (1, left)):
@@ -275,11 +275,11 @@
     for unit in range(1, 4):
         ring(1, unit)
     relays = []
-    for i in range(SPAN):
+    for turn, i in enumerate((0, 2, 4, 6, 1, 3, 5, 7)):
         source = lax.rem(slot + 8 - i, 8)
-        across[0][i].wait_recv()
-        across[1][i].wait_recv()
-        if i % 2 == 0:
+        across[0][turn].wait_recv()
+        across[1][turn].wait_recv()
+        if turn % 2 == 0:
             target, lane = right, lax.rem(x + 3, 4)
         else:
             target, lane = left, lax.rem(x + 1, 4)
@@ -289,8 +289,8 @@
                 f_s.at[i], f_r.at[i], "head", target,
             )
         )
-        if i % 2:
-            ring(2, i // 2)
+        if turn % 2:
+            ring(2, turn // 2)
     own[0].wait()
     own[1].wait()
     for copy in relays + pending[:SPAN - 1]:

time: 102 us -> 102 us (level)
  no operation moved by 1% of the time
where the time goes in v6:
time: 102 us
  Pallas kernels  101 us (99%)
    pallas_call x1, Pallas kernels, body(): pl.pallas_call(attend_kernel, out_shape=(shaped((2, 4, 2, 16, 128)), shap...  99.6 us

profile of v6, /device:TPU:1, one launch (start us, length us, event | category | flops | bytes accessed | tf_op | source)
XLA Modules:
  0.0 102.0 jit_solution(13635810616991494116)
XLA Ops:
  0.6 99.6 %shard_map.138 = (bf16[2,4,2,16,128]{4,3,2,1,0:T(8,128)(2,1)}, bf16[2,4,3,16,128]{4,3,2,1,0:T(8,128)(2,1)}, bf16[2,4,3,16,128]{4,3,2,1,0:T(8,128)(2,1)}, f32[32,128]{1,0:T(8,128)}) custom-call(s32[1,2]{1,0:T(1,128)} %starts_ref.1, bf16[576,128]{1,0:T(8,128)(2,1)} %bitcast.6, bf16[40,1024]{1,0:T(8,128)(2,1)} %bitcast.8, bf16[128,2560]{1,0:T(8,128)(2,1)} %cot_ref.1, ...), custom_call_target="tpu_custom_call" | custom-call | tf_op jit(solution)/shard_map/pallas_call | solution.py:539
  100.2 1.8 %shard_map.139 = (f32[32,1536]{1,0:T(8,128)}, f32[32,1536]{1,0:T(8,128)}, f32[32,1024]{1,0:T(8,128)}, f32[32,40]{1,0:T(8,128)}) custom-call(bf16[2,4,2,16,128]{4,3,2,1,0:T(8,128)(2,1)} %get-tuple-element.12.full_e, bf16[2,4,3,16,128]{4,3,2,1,0:T(8,128)(2,1)} %get-tuple-element.13.full_b, bf16[2,4,3,16,128]{4,3,2,1,0:T(8,128)(2,1)} %get-tuple-element.14.full_a, ...), custom_call_target="tpu_custom_call" | custom-call | tf_op jit(solution)/shard_map/pallas_call | solution.py:581
